TPU v7x, 32 devices: a whole 2x2x4 slice. The times are simulated.
32 devices in a mesh: group: 2 (over y), dp: 4 (over x, core), seq: 4 (over z).
Axes of the slice: x: 2, y: 2, z: 4, core: 2. Of those that a mesh axis runs over, the one named last changes fastest.
Arguments:
- tokens: bfloat16 [8, 1024, 4096], P(('group', 'dp'), 'seq'), parts along dimension 0, may hold values from -6 to 6
- norm_gain: bfloat16 [4096], replicated, may hold values from 0.099609375 to 1.8984375
- qkv_weight: bfloat16 [4096, 3072], P('dp'), may hold values from -4 to 4, as said below
- doc_ids: int32 [8, 1024], P(('group', 'dp'), 'seq'), parts along dimension 0, may hold values from 0 to 5, never falling along the last dimension, each value on 1 to 512 neighbouring positions
Outputs:
- attended: bfloat16 [8, 1024, 2048], P(('group', 'dp'), 'seq'), parts along dimension 0
There are 2 independent parts, one for each index of `group`. A program takes and returns all parts, laid end to end along the dimension named above; an argument that names none is the same for every part. Nothing has to cross between parts.
Inputs may be any that keep to these rules, and one draw needn't show every extreme that they name: `qkv_weight`: in the hidden draw query heads lie close to multiples of their key head. `doc_ids`: ids never fall along a sequence; a document holds at most 512 positions.
All inputs are finite; a program needn't handle non-finite values.
Results may differ from a plain program's by a relative error of at most 0.0075.
Values may be sent and summed in bfloat16 or wider, within the bound.
No kernel may reach another device: no remote copies, remote signals or barrier semaphores. Data moves between devices by JAX's collectives and lax.ppermute only.
A program may use at most 128 MiB of HBM per device.

v0:
```python
import jax
import jax.numpy as jnp
from jax import lax
from jax.sharding import PartitionSpec as P

HD = 128
QH = 16
KVH = 4
QW = 2048
KW = 512


def rms_norm(rows, gain):
    values = rows.astype(jnp.float32)
    scale = lax.rsqrt(jnp.mean(values * values, axis=-1, keepdims=True) + 1e-05)
    return (values * scale * gain.astype(jnp.float32)).astype(jnp.bfloat16)


def rotate(heads, places):
    half = heads.shape[-1] // 2
    freqs = 500000.0 ** (-2.0 * jnp.arange(half, dtype=jnp.float32) / heads.shape[-1])
    angles = places[:, None] * freqs[None, :]
    cosine = jnp.cos(angles)[:, None, :]
    sine = jnp.sin(angles)[:, None, :]
    first = heads[..., :half]
    second = heads[..., half:]
    return jnp.concatenate(
        [first * cosine - second * sine, second * cosine + first * sine], axis=-1
    )


def attend(queries, keys, values, docs):
    length = queries.shape[0]
    local_q = queries.shape[1]
    local_kv = keys.shape[1]
    share = local_q // local_kv
    queries = queries.reshape(length, local_kv, share, HD)
    block = min(512, length)
    scale = 1.0 / HD**0.5
    cols = jnp.arange(length, dtype=jnp.int32)

    def one_block(index):
        start = index * block
        qblock = lax.dynamic_slice_in_dim(queries, start, block, 0)
        scores = (
            jnp.einsum("qkgd,tkd->kgqt", qblock, keys, preferred_element_type=jnp.float32) * scale
        )
        rowpos = start + jnp.arange(block, dtype=jnp.int32)
        rowdoc = lax.dynamic_slice_in_dim(docs, start, block, 0)
        allow = (cols[None, :] <= rowpos[:, None]) & (docs[None, :] == rowdoc[:, None])
        scores = jnp.where(allow[None, None], scores, -1e30)
        peak = jnp.max(scores, axis=-1, keepdims=True)
        expo = jnp.where(allow[None, None], jnp.exp(scores - peak), 0.0)
        total = jnp.sum(expo, axis=-1)
        weights = expo.astype(jnp.bfloat16)
        outs = jnp.einsum("kgqt,tkd->qkgd", weights, values, preferred_element_type=jnp.float32)
        outs = outs / jnp.transpose(total, (2, 0, 1))[..., None]
        return outs.reshape(block, local_q * HD).astype(jnp.bfloat16)

    result = lax.map(one_block, jnp.arange(length // block, dtype=jnp.int32))
    return result.reshape(length, local_q * HD)


def local(tokens, norm_gain, qkv_weight, doc_ids):
    count = lax.axis_size("seq")
    rank = lax.axis_index("seq")
    tok = tokens.shape[1]
    length = tok * count
    local_q = QH // count
    normed = rms_norm(tokens[0], norm_gain)
    all_docs = lax.all_gather(doc_ids, "seq", axis=1, tiled=True)[0]
    proj = jnp.dot(
        normed,
        lax.all_gather(qkv_weight, "dp", axis=0, tiled=True),
        preferred_element_type=jnp.float32,
    )
    places = (rank * tok + jnp.arange(tok, dtype=jnp.int32)).astype(jnp.float32)
    queries = rotate(proj[:, :QW].reshape(tok, QH, HD), places).astype(jnp.bfloat16)
    keys = rotate(proj[:, QW : QW + KW].reshape(tok, KVH, HD), places).astype(jnp.bfloat16)
    values = proj[:, QW + KW :].reshape(tok, KVH, HD).astype(jnp.bfloat16)
    slots = max(KVH, count)
    if slots > KVH:
        keys = jnp.repeat(keys, slots // KVH, axis=1)
        values = jnp.repeat(values, slots // KVH, axis=1)
    q_sent = queries.reshape(tok, count, local_q * HD)
    q_got, k_got, v_got = (
        lax.all_to_all(q_sent, "seq", split_axis=1, concat_axis=0, tiled=True),
        lax.all_to_all(keys, "seq", split_axis=1, concat_axis=0, tiled=True),
        lax.all_to_all(values, "seq", split_axis=1, concat_axis=0, tiled=True),
    )
    q_heads = q_got.reshape(length, local_q, HD)
    outputs = attend(q_heads, k_got, v_got, all_docs)
    back = outputs.reshape(count, tok, local_q * HD)
    return lax.all_to_all(back, "seq", split_axis=0, concat_axis=2, tiled=True)


def solution(mesh):
    in_specs = (P(("group", "dp"), "seq", None), P(), P("dp", None), P(("group", "dp"), "seq"))
    out_specs = P(("group", "dp"), "seq", None)
    return jax.shard_map(local, mesh=mesh, in_specs=in_specs, out_specs=out_specs, check_vma=False)
```

profile of v0, /device:TPU:0, one launch (start us, length us, event | category | flops | bytes accessed | tf_op | source)
XLA Modules:
  0.0 297.0 jit_solution(6609023048014826242)
XLA Ops:
  6.5 0.7 all-gather.2.cloned.1.call-update
  7.3 0.8 copy-done.1
  9.0 157.5 %all-gather.2.cloned.1.call-done = bf16[4096,3072]{1,0:T(8,128)(2,1)} async-done(((bf16[1024,3072]{1,0:T(8,128)(2,1)}), bf16[4096,3072]{1,0:T(8,128)(2,1)}) %all-gather.2.cloned.1.call-update) | async-done | bytes 25165840 | tf_op jit(solution)/shard_map/all_gather | solution.py:74
  166.4 11.6 %fusion.24 = f32[256,3072]{1,0:T(8,128)S(1)} fusion(bf16[4096,3072]{1,0:T(8,128)(2,1)} %all-gather.2.cloned.1.call-done, bf16[1,256,4096]{2,1,0:T(8,128)(2,1)S(1)} %copy-done.1, f32[4096]{0:T(1024)S(1)} %convert_element_type.47, f32[256]{0:T(256)S(1)} %add_rsqrt_fusion), kind=kOutput, calls=%fused_computation.28 | convolution fusion | flops 6446645248 | bytes 30426112 | tf_op jit(solution)/shard_map/dot_general | solution.py:72
  178.1 1.6 slice.29
  179.7 0.7 copy-done
  180.4 0.8 copy_bitcast_fusion.2
  181.2 2.0 copy.35
  183.2 4.6 %all-to-all-start.2 = ((bf16[256,4,128]{2,0,1:T(8,128)(2,1)}), bf16[256,4,128]{2,0,1:T(8,128)(2,1)S(1)}, u32[]{:S(2)}, u32[]{:S(2)}) async-start(bf16[256,4,128]{2,0,1:T(8,128)(2,1)} %copy_bitcast_fusion.2), calls=%async_computation.2 | async-start | bytes 524288 | tf_op jit(solution)/shard_map/all_to_all | solution.py:89
  188.1 1.1 pad_maximum_fusion
  189.2 7.9 %all-to-all-done.2 = bf16[256,4,128]{2,0,1:T(8,128)(2,1)S(1)} async-done(((bf16[256,4,128]{2,0,1:T(8,128)(2,1)}), bf16[256,4,128]{2,0,1:T(8,128)(2,1)S(1)}, u32[]{:S(2)}, u32[]{:S(2)}) %all-to-all-start.2) | async-done | bytes 262176 | tf_op jit(solution)/shard_map/all_to_all | solution.py:89
  197.1 3.5 %all-to-all-start = ((bf16[256,4,512]{0,2,1:T(8,128)(2,1)}), bf16[256,4,512]{0,2,1:T(8,128)(2,1)S(1)}, u32[]{:S(2)}, u32[]{:S(2)}) async-start(bf16[256,4,512]{0,2,1:T(8,128)(2,1)} %bitcast.3), calls=%async_computation | async-start | bytes 2097152 | tf_op jit(solution)/shard_map/all_to_all | solution.py:87
  201.5 0.9 pad_maximum_fusion.1
  202.4 22.4 %all-to-all-done = bf16[256,4,512]{0,2,1:T(8,128)(2,1)S(1)} async-done(((bf16[256,4,512]{0,2,1:T(8,128)(2,1)}), bf16[256,4,512]{0,2,1:T(8,128)(2,1)S(1)}, u32[]{:S(2)}, u32[]{:S(2)}) %all-to-all-start) | async-done | bytes 1048608 | tf_op jit(solution)/shard_map/all_to_all | solution.py:87
  224.8 3.4 %all-to-all-start.1 = ((bf16[256,4,128]{2,0,1:T(8,128)(2,1)}), bf16[256,4,128]{2,0,1:T(8,128)(2,1)S(1)}, u32[]{:S(2)}, u32[]{:S(2)}) async-start(bf16[256,4,128]{2,0,1:T(8,128)(2,1)} %pad_maximum_fusion.1), calls=%async_computation.1 | async-start | bytes 524288 | tf_op jit(solution)/shard_map/all_to_all | solution.py:88
  228.2 11.3 %all_gather.6 = s32[1,1024]{1,0:T(1,128)S(1)} all-gather(s32[1,256]{1,0:T(1,128)S(1)} %copy-done.5), channel_id=1, replica_groups=mesh['group'=2,'dp'=4,'seq'=4] {'seq'}, dimensions={1}, use_global_device_ids=true | all-gather | bytes 5120 | tf_op jit(solution)/shard_map/all_gather | solution.py:71
  239.6 1.8 copy.31
  241.4 0.5 copy.24
  242.2 19.8 %while.11 = (s32[]{:T(128)}, bf16[2,512,512]{2,1,0:T(8,128)(2,1)S(1)}, s32[2]{0:T(128)S(1)}, s32[1,1024]{1,0:T(1,128)S(1)}, s32[1024]{0:T(1024)S(1)}, /*index=5*...) while((s32[]{:T(128)}, ...), condition=%wide.region_4.5_spmd.clone, body=%wide.region_1.4_spmd.clone.sunk | while | flops 1103098368 | bytes 33085660 | solution.py:60
  242.2 0.6 dynamic_slice.18
  243.6 0.5 fusion.40
  244.3 1.9 fusion.41
  246.2 2.9 fusion.42
  249.1 2.8 divide_convert_fusion.2
  252.1 0.6 dynamic_slice.18
  253.5 0.5 fusion.40
  254.2 1.9 fusion.41
  256.1 2.9 fusion.42
  259.0 2.8 divide_convert_fusion.2
  262.0 26.1 %all_to_all.69 = bf16[4,256,512]{2,1,0:T(8,128)(2,1)S(1)} all-to-all(bf16[4,256,512]{2,1,0:T(8,128)(2,1)S(1)} %bitcast.127), channel_id=1, replica_groups=mesh['group'=2,'dp'=4,'seq'=4] {'seq'}, dimensions={0} | all-to-all | bytes 2097152 | tf_op jit(solution)/shard_map/all_to_all | solution.py:94
  288.2 0.5 copy.33
  288.7 1.4 copy.34
  (41 shorter events, 3.4 us)
Async XLA Ops:
  6.5 0.7 copy-start.4
  6.5 1.6 copy-start.1
  6.5 159.9 %all-gather.2.cloned.1.call-start = ((), (), s32[]{:S(2)}) async-start(), calls=%async_computation.4 | async-start | bytes 31457280 | tf_op jit(solution)/shard_map/all_gather | solution.py:74
  178.1 2.3 copy-start
  181.2 19.6 %slice-start = ((f32[256,3072]{1,0:T(8,128)}), f32[256,512]{1,0:T(8,128)S(1)}, s32[]{:S(2)}) async-start(f32[256,3072]{1,0:T(8,128)} %copy-done), calls=%async_computation.5 | async-start | bytes 1048576 | tf_op jit(solution)/shard_map/slice | solution.py:79
  183.2 13.9 %all-to-all-start.2 = ((bf16[256,4,128]{2,0,1:T(8,128)(2,1)}), bf16[256,4,128]{2,0,1:T(8,128)(2,1)S(1)}, u32[]{:S(2)}, u32[]{:S(2)}) async-start(bf16[256,4,128]{2,0,1:T(8,128)(2,1)} %copy_bitcast_fusion.2), calls=%async_computation.2 | async-start | bytes 524288 | tf_op jit(solution)/shard_map/all_to_all | solution.py:89
  188.1 40.1 %copy-start.5 = (s32[1,256]{1,0:T(1,128)S(1)}, s32[1,256]{1,0:T(1,128)}, u32[]{:S(2)}) copy-start(s32[1,256]{1,0:T(1,128)} %param.9) | copy-start | bytes 3076
  197.1 27.7 %copy-start.2 = (bf16[256,4,128]{2,0,1:T(8,128)(2,1)}, bf16[256,4,128]{2,0,1:T(8,128)(2,1)S(1)}, u32[]{:S(2)}) copy-start(bf16[256,4,128]{2,0,1:T(8,128)(2,1)S(1)} %all-to-all-done.2) | copy-start | bytes 786436
  197.1 27.7 %all-to-all-start = ((bf16[256,4,512]{0,2,1:T(8,128)(2,1)}), bf16[256,4,512]{0,2,1:T(8,128)(2,1)S(1)}, u32[]{:S(2)}, u32[]{:S(2)}) async-start(bf16[256,4,512]{0,2,1:T(8,128)(2,1)} %bitcast.3), calls=%async_computation | async-start | bytes 2097152 | tf_op jit(solution)/shard_map/all_to_all | solution.py:87
  224.8 17.4 %all-to-all-start.1 = ((bf16[256,4,128]{2,0,1:T(8,128)(2,1)}), bf16[256,4,128]{2,0,1:T(8,128)(2,1)S(1)}, u32[]{:S(2)}, u32[]{:S(2)}) async-start(bf16[256,4,128]{2,0,1:T(8,128)(2,1)} %pad_maximum_fusion.1), calls=%async_computation.1 | async-start | bytes 524288 | tf_op jit(solution)/shard_map/all_to_all | solution.py:88
  246.1 2.9 copy-start.3
  256.1 2.9 copy-start.3
Sparse Core Ops, SparseCore 0:
  8.9 157.4 all-gather.1
where the time goes:
time: 297 us
  waiting for transfers between devices  189 us (64%)
  blocking collectives  37.5 us (13%)
  matrix products  20.9 us (7%)
  between operations  13.6 us (5%)
  local copies, waits for them, and re-layouts  13.5 us (5%)
  starting transfers between devices  11.5 us (4%)
  other arithmetic  10.1 us (3%)
    all_gather x1, waiting for transfers between devices, local(): lax.all_gather(qkv_weight, 'dp', axis=0, tiled=True)  157 us
    all_to_all x1, blocking collectives, local(): return lax.all_to_all(back, 'seq', split_axis=0, concat_axis=2, tiled=True)  26.1 us
    all_to_all x1, waiting for transfers between devices, local(): lax.all_to_all(q_sent, 'seq', split_axis=1, concat_axis=0, tiled=True)  22.4 us
    dot_general x1, matrix products, local(): jnp.dot(normed, lax.all_gather(qkv_weight, 'dp', axis=0, tiled=True), pre...  11.6 us
    all_gather x1, blocking collectives, local(): all_docs = lax.all_gather(doc_ids, 'seq', axis=1, tiled=True)[0]  11.3 us
    all_to_all x1, waiting for transfers between devices, local(): lax.all_to_all(values, 'seq', split_axis=1, concat_axis=0, tiled=True)  7.93 us
  transfers between devices with their start and end apart: 4, of which 3 were waited for; matrix products, arithmetic and copies ran while one was open for 2% of the time, Pallas kernels for 0%

commit v1 on v0

v1 whole, which is shorter than its diff:
```python
import functools
import math

import jax
import jax.numpy as jnp
from jax import lax
from jax.experimental import pallas as pl
from jax.experimental.pallas import tpu as pltpu
from jax.sharding import PartitionSpec as P

HD = 128
QH = 16
KVH = 4
QW = 2048
KW = 512
SHARE = QH // KVH
GW = SHARE * HD
Q_CHUNKS = 2
EXP2_SCALE = math.log2(math.e) / math.sqrt(HD)


def norm_kernel(order_ref, tok_ref, gain_ref, *out_refs):
    depth = out_refs[0].shape[1] // 2
    values = tok_ref[...].astype(jnp.float32)
    scale = lax.rsqrt(jnp.mean(values * values, axis=-1, keepdims=True) + 1e-05)
    for place, out_ref in enumerate(out_refs):
        for half in range(2):
            start = pl.multiple_of(order_ref[2 * place + half] * depth, 128)
            piece = tok_ref[:, pl.ds(start, depth)].astype(jnp.float32)
            gain = gain_ref[:, pl.ds(start, depth)].astype(jnp.float32)
            out_ref[:, half * depth : (half + 1) * depth] = (piece * scale * gain).astype(
                jnp.bfloat16
            )


def norm_blocks(rows, gain, order, depth):
    tok, width = rows.shape
    chips = order.shape[0] // 2
    step = min(64, tok)
    return pl.pallas_call(
        norm_kernel,
        out_shape=[jax.ShapeDtypeStruct((tok, 2 * depth), jnp.bfloat16)] * chips,
        grid_spec=pltpu.PrefetchScalarGridSpec(
            num_scalar_prefetch=1,
            grid=(tok // step,),
            in_specs=[
                pl.BlockSpec((step, width), lambda i, order: (i, 0)),
                pl.BlockSpec((1, width), lambda i, order: (0, 0)),
            ],
            out_specs=[pl.BlockSpec((step, 2 * depth), lambda i, order: (i, 0))] * chips,
        ),
        name="norm_blocks",
    )(order, rows, gain.reshape(1, width))


def part_kernel(rows_ref, near_ref, far_ref, out_ref):
    depth = near_ref.shape[0]
    total = jnp.dot(rows_ref[:, :depth], near_ref[...], preferred_element_type=jnp.float32)
    total += jnp.dot(rows_ref[:, depth:], far_ref[...], preferred_element_type=jnp.float32)
    out_ref[...] = total.astype(out_ref.dtype)


def part_product(rows, near, far, first, width, dtype, tile=512):
    tok = rows.shape[0]
    depth = near.shape[0]
    base = first // tile
    weight_spec = pl.BlockSpec((depth, tile), lambda i: (0, base + i))
    return pl.pallas_call(
        part_kernel,
        out_shape=jax.ShapeDtypeStruct((tok, width), dtype),
        grid=(width // tile,),
        in_specs=[pl.BlockSpec((tok, 2 * depth), lambda i: (0, 0)), weight_spec, weight_spec],
        out_specs=pl.BlockSpec((tok, tile), lambda i: (0, i)),
        name="part_product",
    )(rows, near, far)


def turn(head, cosine, sine):
    return head * cosine + pltpu.roll(head, HD // 2, 1) * sine


def kv_kernel(cos_ref, sin_ref, own_ref, *refs):
    *got_refs, out_ref = refs
    total = own_ref[...]
    for got_ref in got_refs:
        total += got_ref[...].astype(jnp.float32)
    for head in range(KVH):
        cut = slice(head * HD, (head + 1) * HD)
        out_ref[:, cut] = turn(total[:, cut], cos_ref[...], sin_ref[...]).astype(jnp.bfloat16)
    out_ref[:, KW:] = total[:, KW:].astype(jnp.bfloat16)


def finish_kv(own, got, cosine, sine):
    tok = own.shape[0]
    return pl.pallas_call(
        kv_kernel,
        out_shape=jax.ShapeDtypeStruct((tok, 2 * KW), jnp.bfloat16),
        grid=(1,),
        in_specs=[pl.BlockSpec((tok, HD), lambda i: (0, 0))] * 2
        + [pl.BlockSpec((tok, 2 * KW), lambda i: (0, QW // (2 * KW)))]
        + [pl.BlockSpec((tok, 2 * KW), lambda i: (0, 0))] * len(got),
        out_specs=pl.BlockSpec((tok, 2 * KW), lambda i: (0, 0)),
        name="finish_kv",
    )(cosine, sine, own, *got)


def attend_kernel(parts, blocks, cos_ref, sin_ref, bias_ref, own_ref, *refs):
    got_refs = refs[:parts]
    key_refs = refs[parts : parts + blocks]
    value_refs = refs[parts + blocks : parts + 2 * blocks]
    out_ref = refs[-1]
    keys = jnp.concatenate([ref[...] for ref in key_refs], axis=0)
    values = jnp.concatenate([ref[...] for ref in value_refs], axis=0)
    values = jnp.concatenate([values, jnp.ones_like(values)], axis=1)
    for head in range(SHARE):
        cut = slice(head * HD, (head + 1) * HD)
        query = own_ref[:, cut]
        for got_ref in got_refs:
            query += got_ref[:, cut].astype(jnp.float32)
        query = turn(query, cos_ref[...], sin_ref[...]).astype(jnp.bfloat16)
        scores = lax.dot_general(
            query, keys, (((1,), (1,)), ((), ())), preferred_element_type=jnp.float32
        )
        scores = scores + bias_ref[...]
        peak = jnp.max(scores, axis=-1, keepdims=True)
        expo = jnp.exp2((scores - peak) * EXP2_SCALE).astype(jnp.bfloat16)
        sums = jnp.dot(expo, values, preferred_element_type=jnp.float32)
        out_ref[:, cut] = (sums[:, :HD] / sums[:, HD:]).astype(jnp.bfloat16)


def attend(own, got, kv_blocks, bias, cosine, sine, first, previous):
    tok = own.shape[0]
    blocks = len(kv_blocks)
    heads = QW // Q_CHUNKS // GW
    base = first // GW
    kv_base = base
    whole = lambda i: (0, 0)
    key_spec = pl.BlockSpec((tok, HD), lambda i: (0, kv_base + i))
    value_spec = pl.BlockSpec((tok, HD), lambda i: (0, KVH + kv_base + i))
    in_specs = [
        pl.BlockSpec((tok, HD), whole),
        pl.BlockSpec((tok, HD), whole),
        pl.BlockSpec((tok, blocks * tok), whole),
        pl.BlockSpec((tok, GW), lambda i: (0, base + i)),
    ]
    in_specs += [pl.BlockSpec((tok, GW), lambda i: (0, i))] * len(got)
    in_specs += [key_spec] * blocks + [value_spec] * blocks
    operands = [cosine, sine, bias, own, *got, *kv_blocks, *kv_blocks]
    aliases = {}
    kernel = functools.partial(attend_kernel, len(got), blocks)
    if previous is not None:
        aliases = {len(operands): 0}
        operands.append(previous)
        in_specs.append(pl.BlockSpec(memory_space=pl.ANY))
    return pl.pallas_call(
        kernel,
        out_shape=jax.ShapeDtypeStruct((tok, QW), jnp.bfloat16),
        grid=(heads,),
        in_specs=in_specs,
        out_specs=pl.BlockSpec((tok, GW), lambda i: (0, base + i)),
        input_output_aliases=aliases,
        name="attend",
    )(*operands)


def local(tokens, norm_gain, qkv_weight, doc_ids):
    count = lax.axis_size("seq")
    rank = lax.axis_index("seq")
    ranks = lax.axis_size("dp")
    place = lax.axis_index("dp")
    chips = ranks // 2
    tok = tokens.shape[1]
    depth = qkv_weight.shape[0]
    hops = -(-(tok * count // 2 - 1) // tok)

    far = lax.ppermute(qkv_weight, "dp", [(i, i ^ 1) for i in range(ranks)])
    near = qkv_weight
    order = jnp.stack(
        [((place + 2 * j) % ranks) ^ half for j in range(chips) for half in range(2)]
    ).astype(jnp.int32)
    mine, *sent = norm_blocks(tokens[0], norm_gain, order, depth)
    guests = [
        lax.ppermute(part, "dp", [(i, (i + 2 * j) % ranks) for i in range(ranks)])
        for j, part in enumerate(sent, 1)
    ]

    half = HD // 2
    places = (rank * tok + jnp.arange(tok, dtype=jnp.int32)).astype(jnp.float32)
    freqs = 500000.0 ** (-2.0 * jnp.arange(half, dtype=jnp.float32) / HD)
    angles = places[:, None] * freqs[None, :]
    cosine = jnp.cos(angles)
    sine = jnp.sin(angles)
    cosine = jnp.concatenate([cosine, cosine], axis=1)
    sine = jnp.concatenate([-sine, sine], axis=1)

    docs = doc_ids[0]
    spots = jnp.arange(tok, dtype=jnp.int32)
    allow = [(spots[None, :] <= spots[:, None]) & (docs[None, :] == docs[:, None])]
    for hop in range(1, hops + 1):
        other = lax.ppermute(doc_ids, "seq", [(i, i + hop) for i in range(count - hop)])[0]
        allow.append((rank >= hop) & (other[None, :] == docs[:, None]))
    bias = jnp.where(jnp.concatenate(allow, axis=1), 0.0, -1e30).astype(jnp.float32)

    own = part_product(mine, near, far, 0, QW + 2 * KW, jnp.float32)

    def home(part, j):
        return lax.ppermute(part, "dp", [(i, (i - 2 * j) % ranks) for i in range(ranks)])

    kv_got = [
        home(part_product(rows, near, far, QW, 2 * KW, jnp.bfloat16), j)
        for j, rows in enumerate(guests, 1)
    ]
    q_step = QW // Q_CHUNKS
    q_got = [
        [
            home(part_product(rows, near, far, chunk * q_step, q_step, jnp.bfloat16), j)
            for j, rows in enumerate(guests, 1)
        ]
        for chunk in range(Q_CHUNKS)
    ]
    block = finish_kv(own, kv_got, cosine, sine)
    kv_blocks = [block]
    for hop in range(hops):
        block = lax.ppermute(block, "seq", [(i, i + 1) for i in range(count - 1)])
        kv_blocks.append(block)
    result = None
    for chunk in range(Q_CHUNKS):
        result = attend(
            own, q_got[chunk], kv_blocks, bias, cosine, sine, chunk * q_step, result
        )
    return result[None]


def solution(mesh):
    in_specs = (P(("group", "dp"), "seq", None), P(), P("dp", None), P(("group", "dp"), "seq"))
    out_specs = P(("group", "dp"), "seq", None)
    return jax.shard_map(local, mesh=mesh, in_specs=in_specs, out_specs=out_specs, check_vma=False)
```

time: 297 us -> 102 us (0.34)
  waiting for transfers between devices: 189 us -> 31.6 us
  Pallas kernels: 0 us -> 39.8 us
  blocking collectives: 37.5 us -> 0 us
  matrix products: 20.9 us -> 0 us
  between operations: 13.6 us -> 0.1 us
  starting transfers between devices: 11.5 us -> 21.2 us
  local copies, waits for them, and re-layouts: 13.5 us -> 5.49 us
  other arithmetic: 10.1 us -> 3.16 us
    all_gather x1 -> x0, waiting for transfers between devices: 157 us -> none  [local(): lax.all_gather(qkv_weight, 'dp', axis=0, tiled=True)]
    pallas_call x0 -> x8, Pallas kernels: none -> 39.8 us  [the longest x4 21.6 us: part_product(): pl.pallas_call(part_kernel, out_shape=jax.ShapeDtypeStruct((tok, width),...]
    ppermute x0 -> x9, waiting for transfers between devices: none -> 31.6 us  [the longest x1 24 us: local(): lax.ppermute(part, 'dp', [(i, (i + 2 * j) % ranks) for i in range(ranks)])]
    all_to_all x3 -> x0, waiting for transfers between devices: 30.4 us -> none  [the longest x1 22.4 us: local(): lax.all_to_all(q_sent, 'seq', split_axis=1, concat_axis=0, tiled=True)]
    all_to_all x1 -> x0, blocking collectives: 26.1 us -> none  [local(): return lax.all_to_all(back, 'seq', split_axis=0, concat_axis=2, tiled=True)]
    ppermute x0 -> x9, starting transfers between devices: none -> 21.2 us  [the longest x2 7.77 us: local(): block = lax.ppermute(block, 'seq', [(i, i + 1) for i in range(count - 1)])]
    dot_general x5 -> x0, matrix products: 20.9 us -> none  [the longest x1 11.6 us: local(): jnp.dot(normed, lax.all_gather(qkv_weight, 'dp', axis=0, tiled=True), pre...]
    all_to_all x3 -> x0, starting transfers between devices: 11.5 us -> none  [the longest x1 4.59 us: local(): lax.all_to_all(values, 'seq', split_axis=1, concat_axis=0, tiled=True)]
  transfers between devices with their start and end apart: 4 -> 9, of which waited for: 3 -> 4; matrix products, arithmetic and copies ran while one was open for 2% -> 4% of each run, Pallas kernels for 0% -> 27%
where the time goes in v1:
time: 102 us; the launch traced here: 101 us
  Pallas kernels  39.8 us (39%)
  waiting for transfers between devices  31.6 us (31%)
  starting transfers between devices  21.2 us (21%)
  local copies, waits for them, and re-layouts  5.49 us (5%)
  other arithmetic  3.16 us (3%)
    ppermute x1, waiting for transfers between devices, local(): lax.ppermute(part, 'dp', [(i, (i + 2 * j) % ranks) for i in range(ranks)])  24 us
    pallas_call x4, Pallas kernels, part_product(): pl.pallas_call(part_kernel, out_shape=jax.ShapeDtypeStruct((tok, width),...  21.6 us
    pallas_call x2, Pallas kernels, attend(): pl.pallas_call(kernel, out_shape=jax.ShapeDtypeStruct((tok, QW), jnp.bflo...  10.9 us
    ppermute x2, starting transfers between devices, local(): block = lax.ppermute(block, 'seq', [(i, i + 1) for i in range(count - 1)])  7.77 us
    ppermute x2, starting transfers between devices, local(): lax.ppermute(doc_ids, 'seq', [(i, i + hop) for i in range(count - hop)])[0]  5.74 us
    ppermute x2, waiting for transfers between devices, local(): block = lax.ppermute(block, 'seq', [(i, i + 1) for i in range(count - 1)])  4.88 us
    pallas_call x1, Pallas kernels, norm_blocks(): pl.pallas_call(norm_kernel, out_shape=[jax.ShapeDtypeStruct((tok, 2 * dep...  4.81 us
    ppermute x3, starting transfers between devices, home(): lax.ppermute(part, 'dp', [(i, (i - 2 * j) % ranks) for i in range(ranks)])  4.73 us
  transfers between devices with their start and end apart: 9, of which 4 were waited for; matrix products, arithmetic and copies ran while one was open for 4% of the time, Pallas kernels for 27%

profile of v1, /device:TPU:0, one launch (start us, length us, event | category | flops | bytes accessed | tf_op | source)
XLA Modules:
  0.0 101.4 jit_solution(16563524194507572538)
XLA Ops:
  0.0 0.5 collective-permute-start.2
  0.5 1.3 %reshape.14.gain_ref = bf16[1,4096]{1,0:T(2,128)(2,1)} reshape(bf16[4096]{0:T(1024)(128)(2,1)} %param.5) | data formatting | bytes 16384 | tf_op jit(solution)/shard_map/reshape | solution.py:53
  1.8 0.6 pad_add_fusion.order_ref
  2.4 4.8 %norm_blocks.1 = (bf16[256,2048]{1,0:T(8,128)(2,1)}, bf16[256,2048]{1,0:T(8,128)(2,1)}) custom-call(s32[4]{0:T(128)} %pad_add_fusion.order_ref, bf16[256,4096]{1,0:T(8,128)(2,1)} %bitcast.9, bf16[1,4096]{1,0:T(2,128)(2,1)} %reshape.14.gain_ref), custom_call_target="tpu_custom_call" | custom-call | tf_op jit(solution)/shard_map/norm_blocks/pallas_call | solution.py:40
  7.2 2.5 %collective-permute-start.3 = (bf16[256,2048]{1,0:T(8,128)(2,1)}, bf16[256,2048]{1,0:T(8,128)(2,1)S(1)}, u32[]{:S(2)}, u32[]{:S(2)}) collective-permute-start(bf16[256,2048]{1,0:T(8,128)(2,1)} %get-tuple-element.8), channel_id=1, source_target_pairs={{0,8},{4,12},{8,0},{12,4},{1,9},{5,13},{9,1},{13,5},{2,10},{6,14},... | collective-permute-start | bytes 3145736 | tf_op jit(solution)/shard_map/ppermute | solution.py:183
  9.7 24.0 %collective-permute-done.3.rows_ref = bf16[256,2048]{1,0:T(8,128)(2,1)S(1)} collective-permute-done((bf16[256,2048]{1,0:T(8,128)(2,1)}, bf16[256,2048]{1,0:T(8,128)(2,1)S(1)}, u32[]{:S(2)}, u32[]{:S(2)}) %collective-permute-start.3) | collective-permute-done | bytes 1048608 | tf_op jit(solution)/shard_map/ppermute | solution.py:183
  33.7 1.0 copy-done
  34.7 4.0 %part_product.6 = bf16[256,1024]{1,0:T(8,128)(2,1)} custom-call(bf16[256,2048]{1,0:T(8,128)(2,1)} %copy-done, bf16[1024,3072]{1,0:T(8,128)(2,1)} %near_ref.7, bf16[1024,3072]{1,0:T(8,128)(2,1)} %collective-permute-done.2.far_ref), custom_call_target="tpu_custom_call" | custom-call | tf_op jit(solution)/shard_map/part_product/pallas_call | solution.py:68
  38.7 1.7 %collective-permute-start.5 = (bf16[256,1024]{1,0:T(8,128)(2,1)}, bf16[256,1024]{1,0:T(8,128)(2,1)S(1)}, u32[]{:S(2)}, u32[]{:S(2)}) collective-permute-start(bf16[256,1024]{1,0:T(8,128)(2,1)} %part_product.6), channel_id=1, source_target_pairs={{0,8},{4,12},{8,0},{12,4},{1,9},{5,13},{9,1},{13,5},{2,10},{6,14},... | collective-permute-start | bytes 1572872 | tf_op jit(solution)/shard_map/ppermute | solution.py:207
  40.5 0.5 fusion.1
  41.1 0.8 pad_maximum_fusion
  41.9 9.4 %part_product.4.own_ref = f32[256,3072]{1,0:T(8,128)} custom-call(bf16[256,2048]{1,0:T(8,128)(2,1)} %get-tuple-element.7.rows_ref, bf16[1024,3072]{1,0:T(8,128)(2,1)} %near_ref.7, bf16[1024,3072]{1,0:T(8,128)(2,1)} %collective-permute-done.2.far_ref), custom_call_target="tpu_custom_call" | custom-call | tf_op jit(solution)/shard_map/part_product/pallas_call | solution.py:68
  51.3 1.4 %collective-permute-done.5.refs_0_ = bf16[256,1024]{1,0:T(8,128)(2,1)S(1)} collective-permute-done((bf16[256,1024]{1,0:T(8,128)(2,1)}, bf16[256,1024]{1,0:T(8,128)(2,1)S(1)}, u32[]{:S(2)}, u32[]{:S(2)}) %collective-permute-start.5) | collective-permute-done | bytes 524320 | tf_op jit(solution)/shard_map/ppermute | solution.py:207
  52.7 0.8 copy-done.5
  53.5 2.5 %finish_kv.1.refs_1_.refs_4_ = bf16[256,1024]{1,0:T(8,128)(2,1)} custom-call(f32[256,128]{1,0:T(8,128)} %get-tuple-element.15.cos_ref, f32[256,128]{1,0:T(8,128)} %get-tuple-element.16.sin_ref, f32[256,3072]{1,0:T(8,128)} %part_product.4.own_ref, bf16[256,1024]{1,0:T(8,128)(2,1)} %copy-done.5), custom_call_target="tpu_custom_call" | custom-call | tf_op jit(solution)/shard_map/finish_kv/pallas_call | solution.py:95
  56.1 3.5 %collective-permute-start.6 = (bf16[256,1024]{1,0:T(8,128)(2,1)}, bf16[256,1024]{1,0:T(8,128)(2,1)S(1)}, u32[]{:S(2)}, u32[]{:S(2)}) collective-permute-start(bf16[256,1024]{1,0:T(8,128)(2,1)} %finish_kv.1.refs_1_.refs_4_), channel_id=1, source_target_pairs={{0,1},{1,2},{2,3},{4,5},{5,6},{6,7},{8,9},{9,10},{10,11},{12,13},{... | collective-permute-start | bytes 1572872 | tf_op jit(solution)/shard_map/ppermute | solution.py:224
  59.5 4.0 %part_product.7 = bf16[256,1024]{1,0:T(8,128)(2,1)} custom-call(bf16[256,2048]{1,0:T(8,128)(2,1)} %copy-done, bf16[1024,3072]{1,0:T(8,128)(2,1)} %near_ref.7, bf16[1024,3072]{1,0:T(8,128)(2,1)} %collective-permute-done.2.far_ref), custom_call_target="tpu_custom_call" | custom-call | tf_op jit(solution)/shard_map/part_product/pallas_call | solution.py:68
  63.6 1.5 %collective-permute-start.8 = (bf16[256,1024]{1,0:T(8,128)(2,1)}, bf16[256,1024]{1,0:T(8,128)(2,1)S(1)}, u32[]{:S(2)}, u32[]{:S(2)}) collective-permute-start(bf16[256,1024]{1,0:T(8,128)(2,1)} %part_product.7), channel_id=1, source_target_pairs={{0,8},{4,12},{8,0},{12,4},{1,9},{5,13},{9,1},{13,5},{2,10},{6,14},... | collective-permute-start | bytes 1572872 | tf_op jit(solution)/shard_map/ppermute | solution.py:207
  65.1 4.9 %collective-permute-done.6.refs_2_.refs_5_ = bf16[256,1024]{1,0:T(8,128)(2,1)S(1)} collective-permute-done((bf16[256,1024]{1,0:T(8,128)(2,1)}, bf16[256,1024]{1,0:T(8,128)(2,1)S(1)}, u32[]{:S(2)}, u32[]{:S(2)}) %collective-permute-start.6) | collective-permute-done | bytes 524320 | tf_op jit(solution)/shard_map/ppermute | solution.py:224
  69.9 4.3 %collective-permute-start.7 = (bf16[256,1024]{1,0:T(8,128)(2,1)S(1)}, bf16[256,1024]{1,0:T(8,128)(2,1)S(1)}, u32[]{:S(2)}, u32[]{:S(2)}) collective-permute-start(bf16[256,1024]{1,0:T(8,128)(2,1)S(1)} %collective-permute-done.6.refs_2_.refs_5_), channel_id=1, source_target_pairs={{0,1},{1,2},{2,3},{4,5},{5,6},{6,7},{8,9},{9,10},{10,11},{12,13},{... | collective-permute-start | bytes 1572872 | tf_op jit(solution)/shard_map/ppermute | solution.py:224
  74.3 4.1 %part_product.5 = bf16[256,1024]{1,0:T(8,128)(2,1)} custom-call(bf16[256,2048]{1,0:T(8,128)(2,1)} %copy-done, bf16[1024,3072]{1,0:T(8,128)(2,1)} %near_ref.7, bf16[1024,3072]{1,0:T(8,128)(2,1)} %collective-permute-done.2.far_ref), custom_call_target="tpu_custom_call" | custom-call | tf_op jit(solution)/shard_map/part_product/pallas_call | solution.py:68
  78.3 1.5 %collective-permute-start.4 = (bf16[256,1024]{1,0:T(8,128)(2,1)}, bf16[256,1024]{1,0:T(8,128)(2,1)S(1)}, u32[]{:S(2)}, u32[]{:S(2)}) collective-permute-start(bf16[256,1024]{1,0:T(8,128)(2,1)} %part_product.5), channel_id=1, source_target_pairs={{0,8},{4,12},{8,0},{12,4},{1,9},{5,13},{9,1},{13,5},{2,10},{6,14},... | collective-permute-start | bytes 1572872 | tf_op jit(solution)/shard_map/ppermute | solution.py:207
  79.8 4.5 %collective-permute-start.1 = (s32[1,256]{1,0:T(1,128)S(1)}, s32[1,256]{1,0:T(1,128)S(1)}, u32[]{:S(2)}, u32[]{:S(2)}) collective-permute-start(s32[1,256]{1,0:T(1,128)S(1)} %copy-done.6), channel_id=1, source_target_pairs={{0,2},{1,3},{4,6},{5,7},{8,10},{9,11},{12,14},{13,15},{16,18},{17,... | collective-permute-start | bytes 3080 | tf_op jit(solution)/shard_map/ppermute | solution.py:200
  84.3 1.3 %collective-permute-start = (s32[1,256]{1,0:T(1,128)S(1)}, s32[1,256]{1,0:T(1,128)S(1)}, u32[]{:S(2)}, u32[]{:S(2)}) collective-permute-start(s32[1,256]{1,0:T(1,128)S(1)} %copy-done.6), channel_id=1, source_target_pairs={{0,1},{1,2},{2,3},{4,5},{5,6},{6,7},{8,9},{9,10},{10,11},{12,13},{... | collective-permute-start | bytes 3080 | tf_op jit(solution)/shard_map/ppermute | solution.py:200
  85.6 1.3 %collective-permute-done = s32[1,256]{1,0:T(1,128)S(1)} collective-permute-done((s32[1,256]{1,0:T(1,128)S(1)}, s32[1,256]{1,0:T(1,128)S(1)}, u32[]{:S(2)}, u32[]{:S(2)}) %collective-permute-start) | collective-permute-done | bytes 1056 | tf_op jit(solution)/shard_map/ppermute | solution.py:200
  86.9 0.2 fusion
  87.1 1.0 add_select_fusion.bias_ref
  88.1 0.8 copy-done.3
  88.9 0.8 copy-done.2
  89.7 5.4 %attend.2.refs_7_ = bf16[256,2048]{1,0:T(8,128)(2,1)} custom-call(f32[256,128]{1,0:T(8,128)} %get-tuple-element.15.cos_ref, f32[256,128]{1,0:T(8,128)} %get-tuple-element.16.sin_ref, f32[256,768]{1,0:T(8,128)} %add_select_fusion.bias_ref, f32[256,3072]{1,0:T(8,128)} %part_product.4.own_ref, bf16[256,1024]{1,0:T(8,128)(2,1)} %copy-done.3, ...), custom_call_target="tpu_custom_call" | custom-call | tf_op jit(solution)/shard_map/attend/pallas_call | solution.py:155
  95.1 0.8 copy-done.4
  95.9 5.5 %attend.3 = bf16[256,2048]{1,0:T(8,128)(2,1)} custom-call(f32[256,128]{1,0:T(8,128)} %get-tuple-element.15.cos_ref, f32[256,128]{1,0:T(8,128)} %get-tuple-element.16.sin_ref, f32[256,768]{1,0:T(8,128)} %add_select_fusion.bias_ref, f32[256,3072]{1,0:T(8,128)} %part_product.4.own_ref, bf16[256,1024]{1,0:T(8,128)(2,1)} %copy-done.4, ...), custom_call_target="tpu_custom_call", output_to_operand_aliasing={{}: (11, {})} | custom-call | tf_op jit(solution)/shard_map/attend/pallas_call | solution.py:155
  (16 shorter events, 0.0 us)
Async XLA Ops:
  0.0 33.7 %collective-permute-start.2 = (bf16[1024,3072]{1,0:T(8,128)(2,1)}, bf16[1024,3072]{1,0:T(8,128)(2,1)}, u32[]{:S(2)}, u32[]{:S(2)}) collective-permute-start(bf16[1024,3072]{1,0:T(8,128)(2,1)} %near_ref.7), channel_id=1, source_target_pairs={{0,4},{4,0},{8,12},{12,8},{1,5},{5,1},{9,13},{13,9},{2,6},{6,2},{1... | collective-permute-start | bytes 18874376 | tf_op jit(solution)/shard_map/ppermute | solution.py:176
  7.2 26.5 %collective-permute-start.3 = (bf16[256,2048]{1,0:T(8,128)(2,1)}, bf16[256,2048]{1,0:T(8,128)(2,1)S(1)}, u32[]{:S(2)}, u32[]{:S(2)}) collective-permute-start(bf16[256,2048]{1,0:T(8,128)(2,1)} %get-tuple-element.8), channel_id=1, source_target_pairs={{0,8},{4,12},{8,0},{12,4},{1,9},{5,13},{9,1},{13,5},{2,10},{6,14},... | collective-permute-start | bytes 3145736 | tf_op jit(solution)/shard_map/ppermute | solution.py:183
  33.7 1.0 copy-start
  38.7 14.0 %collective-permute-start.5 = (bf16[256,1024]{1,0:T(8,128)(2,1)}, bf16[256,1024]{1,0:T(8,128)(2,1)S(1)}, u32[]{:S(2)}, u32[]{:S(2)}) collective-permute-start(bf16[256,1024]{1,0:T(8,128)(2,1)} %part_product.6), channel_id=1, source_target_pairs={{0,8},{4,12},{8,0},{12,4},{1,9},{5,13},{9,1},{13,5},{2,10},{6,14},... | collective-permute-start | bytes 1572872 | tf_op jit(solution)/shard_map/ppermute | solution.py:207
  52.7 0.8 copy-start.5
  56.1 13.9 %collective-permute-start.6 = (bf16[256,1024]{1,0:T(8,128)(2,1)}, bf16[256,1024]{1,0:T(8,128)(2,1)S(1)}, u32[]{:S(2)}, u32[]{:S(2)}) collective-permute-start(bf16[256,1024]{1,0:T(8,128)(2,1)} %finish_kv.1.refs_1_.refs_4_), channel_id=1, source_target_pairs={{0,1},{1,2},{2,3},{4,5},{5,6},{6,7},{8,9},{9,10},{10,11},{12,13},{... | collective-permute-start | bytes 1572872 | tf_op jit(solution)/shard_map/ppermute | solution.py:224
  63.6 16.3 %copy-start.6 = (s32[1,256]{1,0:T(1,128)S(1)}, s32[1,256]{1,0:T(1,128)}, u32[]{:S(2)}) copy-start(s32[1,256]{1,0:T(1,128)} %param.7) | copy-start | bytes 3076
  63.6 24.5 %collective-permute-start.8 = (bf16[256,1024]{1,0:T(8,128)(2,1)}, bf16[256,1024]{1,0:T(8,128)(2,1)S(1)}, u32[]{:S(2)}, u32[]{:S(2)}) collective-permute-start(bf16[256,1024]{1,0:T(8,128)(2,1)} %part_product.7), channel_id=1, source_target_pairs={{0,8},{4,12},{8,0},{12,4},{1,9},{5,13},{9,1},{13,5},{2,10},{6,14},... | collective-permute-start | bytes 1572872 | tf_op jit(solution)/shard_map/ppermute | solution.py:207
  69.9 8.4 %copy-start.1 = (bf16[256,1024]{1,0:T(8,128)(2,1)}, bf16[256,1024]{1,0:T(8,128)(2,1)S(1)}, u32[]{:S(2)}) copy-start(bf16[256,1024]{1,0:T(8,128)(2,1)S(1)} %collective-permute-done.6.refs_2_.refs_5_) | copy-start | bytes 1572868
  69.9 18.1 %collective-permute-start.7 = (bf16[256,1024]{1,0:T(8,128)(2,1)S(1)}, bf16[256,1024]{1,0:T(8,128)(2,1)S(1)}, u32[]{:S(2)}, u32[]{:S(2)}) collective-permute-start(bf16[256,1024]{1,0:T(8,128)(2,1)S(1)} %collective-permute-done.6.refs_2_.refs_5_), channel_id=1, source_target_pairs={{0,1},{1,2},{2,3},{4,5},{5,6},{6,7},{8,9},{9,10},{10,11},{12,13},{... | collective-permute-start | bytes 1572872 | tf_op jit(solution)/shard_map/ppermute | solution.py:224
  78.3 16.8 %collective-permute-start.4 = (bf16[256,1024]{1,0:T(8,128)(2,1)}, bf16[256,1024]{1,0:T(8,128)(2,1)S(1)}, u32[]{:S(2)}, u32[]{:S(2)}) collective-permute-start(bf16[256,1024]{1,0:T(8,128)(2,1)} %part_product.5), channel_id=1, source_target_pairs={{0,8},{4,12},{8,0},{12,4},{1,9},{5,13},{9,1},{13,5},{2,10},{6,14},... | collective-permute-start | bytes 1572872 | tf_op jit(solution)/shard_map/ppermute | solution.py:207
  79.8 5.8 %collective-permute-start.1 = (s32[1,256]{1,0:T(1,128)S(1)}, s32[1,256]{1,0:T(1,128)S(1)}, u32[]{:S(2)}, u32[]{:S(2)}) collective-permute-start(s32[1,256]{1,0:T(1,128)S(1)} %copy-done.6), channel_id=1, source_target_pairs={{0,2},{1,3},{4,6},{5,7},{8,10},{9,11},{12,14},{13,15},{16,18},{17,... | collective-permute-start | bytes 3080 | tf_op jit(solution)/shard_map/ppermute | solution.py:200
  84.3 2.6 %collective-permute-start = (s32[1,256]{1,0:T(1,128)S(1)}, s32[1,256]{1,0:T(1,128)S(1)}, u32[]{:S(2)}, u32[]{:S(2)}) collective-permute-start(s32[1,256]{1,0:T(1,128)S(1)} %copy-done.6), channel_id=1, source_target_pairs={{0,1},{1,2},{2,3},{4,5},{5,6},{6,7},{8,9},{9,10},{10,11},{12,13},{... | collective-permute-start | bytes 3080 | tf_op jit(solution)/shard_map/ppermute | solution.py:200
  88.0 0.8 copy-start.3
  88.9 0.8 copy-start.2
  95.1 0.8 copy-start.4

commit v2 on v0

v2 whole, which is shorter than its diff:
```python
import functools
import math

import jax
import jax.numpy as jnp
from jax import lax
from jax.experimental import pallas as pl
from jax.experimental.pallas import tpu as pltpu
from jax.sharding import PartitionSpec as P


HD = 128
QH = 16
KVH = 4
QW = 2048
KW = 512
SHARE = QH // KVH
EXP2_SCALE = math.log2(math.e) / math.sqrt(HD)
HALVES = 2

ANY = pl.BlockSpec(memory_space=pl.ANY)


def row_scale(values):
    return lax.rsqrt(jnp.mean(values * values, axis=-1, keepdims=True) + 1e-05)


def write_blocks(tok_ref, gain_ref, scale, out_ref, chip, core):
    depth = out_ref.shape[1] // 2
    for half in range(2):
        block = 2 * chip + (core if half == 0 else 1 - core)
        cut = pl.ds(pl.multiple_of(block * depth, 128), depth)
        piece = tok_ref[:, cut].astype(jnp.float32) * scale
        piece = piece * gain_ref[cut].astype(jnp.float32)[None, :]
        out_ref[:, half * depth : (half + 1) * depth] = piece.astype(jnp.bfloat16)


def norm_kernel(chips, tok_ref, gain_ref, *out_refs):
    place = lax.axis_index("dp")
    scale = row_scale(tok_ref[...].astype(jnp.float32))
    for j, out_ref in enumerate(out_refs, 1):
        chip = lax.rem(lax.div(place, 2) + j, chips)
        write_blocks(tok_ref, gain_ref, scale, out_ref, chip, lax.rem(place, 2))


def norm_sent(rows, gain, part, depth, chips):
    tok, width = rows.shape
    step = tok // HALVES
    return pl.pallas_call(
        functools.partial(norm_kernel, chips),
        out_shape=[jax.ShapeDtypeStruct((step, 2 * depth), jnp.bfloat16)] * (chips - 1),
        grid=(1,),
        in_specs=[
            pl.BlockSpec((step, width), lambda i: (part, 0)),
            pl.BlockSpec((width,), lambda i: (0,)),
        ],
        out_specs=[pl.BlockSpec((step, 2 * depth), lambda i: (0, 0))] * (chips - 1),
        compiler_params=pltpu.CompilerParams(vmem_limit_bytes=64 * 1024 * 1024),
        name="norm_sent",
    )(rows, gain)


def weight_copies(first, width, tile, near_hbm, far_hbm, near, far, sems):
    copies = []
    for c in range(width // tile):
        cut = pl.ds(first + c * tile, tile)
        kept = pl.ds(c * tile, tile)
        copies.append(
            (
                pltpu.make_async_copy(near_hbm.at[:, cut], near.at[:, kept], sems.at[c, 0]),
                pltpu.make_async_copy(far_hbm.at[:, cut], far.at[:, kept], sems.at[c, 1]),
            )
        )
    for pair in copies:
        for copy in pair:
            copy.start()
    return copies


def multiply(rows, copies, tile, near, far, out_ref):
    depth = near.shape[0]
    for c, (near_copy, far_copy) in enumerate(copies):
        kept = slice(c * tile, (c + 1) * tile)
        near_copy.wait()
        total = jnp.dot(rows[:, :depth], near[:, kept], preferred_element_type=jnp.float32)
        far_copy.wait()
        total += jnp.dot(rows[:, depth:], far[:, kept], preferred_element_type=jnp.float32)
        out_ref[:, kept] = total.astype(out_ref.dtype)


def own_kernel(tile, tok_ref, gain_ref, near_hbm, far_hbm, out_ref, near, far, mine, sems):
    copies = weight_copies(0, out_ref.shape[1], tile, near_hbm, far_hbm, near, far, sems)
    place = lax.axis_index("dp")
    scale = row_scale(tok_ref[...].astype(jnp.float32))
    write_blocks(tok_ref, gain_ref, scale, mine, lax.div(place, 2), lax.rem(place, 2))
    multiply(mine, copies, tile, near, far, out_ref)


def own_product(rows, gain, near, far, tile=512):
    tok, width = rows.shape
    depth, columns = near.shape
    whole = lambda i: (0, 0)
    return pl.pallas_call(
        functools.partial(own_kernel, tile),
        out_shape=jax.ShapeDtypeStruct((tok, columns), jnp.float32),
        grid=(1,),
        in_specs=[pl.BlockSpec((tok, width), whole), pl.BlockSpec((width,), lambda i: (0,)), ANY, ANY],
        out_specs=pl.BlockSpec((tok, columns), whole),
        scratch_shapes=[
            pltpu.VMEM((depth, columns), jnp.bfloat16),
            pltpu.VMEM((depth, columns), jnp.bfloat16),
            pltpu.VMEM((tok, 2 * depth), jnp.bfloat16),
            pltpu.SemaphoreType.DMA((columns // tile, 2)),
        ],
        compiler_params=pltpu.CompilerParams(vmem_limit_bytes=64 * 1024 * 1024),
        name="own_product",
    )(rows, gain, near, far)


def guest_kernel(first, tile, rows_hbm, near_hbm, far_hbm, out_ref, rows, near, far, sems, sem):
    rows_copy = pltpu.make_async_copy(rows_hbm, rows, sem)
    rows_copy.start()
    copies = weight_copies(first, out_ref.shape[1], tile, near_hbm, far_hbm, near, far, sems)
    rows_copy.wait()
    multiply(rows, copies, tile, near, far, out_ref)


def guest_product(rows, near, far, first, width, tile=512):
    tok = rows.shape[0]
    depth = near.shape[0]
    return pl.pallas_call(
        functools.partial(guest_kernel, first, tile),
        out_shape=jax.ShapeDtypeStruct((tok, width), jnp.bfloat16),
        grid=(1,),
        in_specs=[ANY, ANY, ANY],
        out_specs=pl.BlockSpec((tok, width), lambda i: (0, 0)),
        scratch_shapes=[
            pltpu.VMEM((tok, 2 * depth), jnp.bfloat16),
            pltpu.VMEM((depth, width), jnp.bfloat16),
            pltpu.VMEM((depth, width), jnp.bfloat16),
            pltpu.SemaphoreType.DMA((width // tile, 2)),
            pltpu.SemaphoreType.DMA,
        ],
        compiler_params=pltpu.CompilerParams(vmem_limit_bytes=64 * 1024 * 1024),
        name="guest_product",
    )(rows, near, far)


def turn(head, cosine, sine):
    return head * cosine + pltpu.roll(head, HD // 2, 1) * sine


def copy_in(sources, targets, sems):
    copies = [
        pltpu.make_async_copy(source, target, sems.at[i])
        for i, (source, target) in enumerate(zip(sources, targets))
    ]
    for copy in copies:
        copy.start()
    return copies


def kv_kernel(count, cos_ref, sin_ref, own_ref, *refs):
    got_hbm, out_ref, got, sems = refs[:count], refs[count], refs[count + 1], refs[count + 2]
    copies = copy_in(got_hbm, [got.at[i] for i in range(count)], sems)
    total = own_ref[...]
    for i, copy in enumerate(copies):
        copy.wait()
        total += got[i].astype(jnp.float32)
    for head in range(KVH):
        cut = slice(head * HD, (head + 1) * HD)
        out_ref[:, cut] = turn(total[:, cut], cos_ref[...], sin_ref[...]).astype(jnp.bfloat16)
    out_ref[:, KW:] = total[:, KW:].astype(jnp.bfloat16)


def finish_kv(own, got, cosine, sine, part):
    step = got[0].shape[0]
    width = 2 * KW
    rows = lambda i: (part, 0)
    return pl.pallas_call(
        functools.partial(kv_kernel, len(got)),
        out_shape=jax.ShapeDtypeStruct((step, width), jnp.bfloat16),
        grid=(1,),
        in_specs=[pl.BlockSpec((step, HD), rows), pl.BlockSpec((step, HD), rows)]
        + [pl.BlockSpec((step, width), lambda i: (part, QW // width))]
        + [ANY] * len(got),
        out_specs=pl.BlockSpec((step, width), lambda i: (0, 0)),
        scratch_shapes=[
            pltpu.VMEM((len(got), step, width), jnp.bfloat16),
            pltpu.SemaphoreType.DMA((len(got),)),
        ],
        compiler_params=pltpu.CompilerParams(vmem_limit_bytes=64 * 1024 * 1024),
        name="finish_kv",
    )(cosine, sine, own, *got)


def attend_kernel(parts, picks, cos_ref, sin_ref, bias_ref, own_ref, *refs):
    blocks = len(picks)
    sources = refs[: parts + blocks]
    out_ref, got, kv, sems = refs[-4:]
    step = got.shape[1]
    targets = [got.at[i] for i in range(parts)]
    targets += [kv.at[pl.ds(i * step, step)] for i in range(blocks)]
    copies = copy_in(sources, targets, sems)
    bias = jnp.concatenate([bias_ref[:, p * step : (p + 1) * step] for p in picks], axis=1)
    for copy in copies:
        copy.wait()
    for group in range(KVH):
        keys = kv[:, group * HD : (group + 1) * HD]
        values = kv[:, KW + group * HD : KW + (group + 1) * HD]
        values = jnp.concatenate([values, jnp.ones_like(values)], axis=1)
        for head in range(group * SHARE, (group + 1) * SHARE):
            cut = slice(head * HD, (head + 1) * HD)
            query = own_ref[:, cut]
            for i in range(parts):
                query += got[i, :, cut].astype(jnp.float32)
            query = turn(query, cos_ref[...], sin_ref[...]).astype(jnp.bfloat16)
            scores = lax.dot_general(
                query, keys, (((1,), (1,)), ((), ())), preferred_element_type=jnp.float32
            )
            scores = scores + bias
            peak = jnp.max(scores, axis=-1, keepdims=True)
            expo = jnp.exp2((scores - peak) * EXP2_SCALE).astype(jnp.bfloat16)
            sums = jnp.dot(expo, values, preferred_element_type=jnp.float32)
            out_ref[:, cut] = (sums[:, :HD] / sums[:, HD:]).astype(jnp.bfloat16)


def attend(own, got, kv_blocks, picks, bias, cosine, sine, part, previous):
    tok = own.shape[0]
    step = tok // HALVES
    blocks = len(picks)
    rows = lambda i: (part, 0)
    in_specs = [
        pl.BlockSpec((step, HD), rows),
        pl.BlockSpec((step, HD), rows),
        pl.BlockSpec((step, bias.shape[1]), rows),
        pl.BlockSpec((step, QW), rows),
    ]
    in_specs += [ANY] * (len(got) + blocks)
    operands = [cosine, sine, bias, own, *got, *kv_blocks]
    aliases = {}
    if previous is not None:
        aliases = {len(operands): 0}
        operands.append(previous)
        in_specs.append(ANY)
    return pl.pallas_call(
        functools.partial(attend_kernel, len(got), picks),
        out_shape=jax.ShapeDtypeStruct((tok, QW), jnp.bfloat16),
        grid=(1,),
        in_specs=in_specs,
        out_specs=pl.BlockSpec((step, QW), rows),
        scratch_shapes=[
            pltpu.VMEM((len(got), step, QW), jnp.bfloat16),
            pltpu.VMEM((blocks * step, 2 * KW), jnp.bfloat16),
            pltpu.SemaphoreType.DMA((len(got) + blocks,)),
        ],
        input_output_aliases=aliases,
        compiler_params=pltpu.CompilerParams(vmem_limit_bytes=64 * 1024 * 1024),
        name="attend",
    )(*operands)


def local(tokens, norm_gain, qkv_weight, doc_ids):
    count = lax.axis_size("seq")
    rank = lax.axis_index("seq")
    ranks = lax.axis_size("dp")
    chips = ranks // 2
    tok = tokens.shape[1]
    depth = qkv_weight.shape[0]
    step = tok // HALVES
    reach = tok * count // 2 - 1
    hops = -(-reach // tok)

    def away(part, j):
        return lax.ppermute(part, "dp", [(i, (i + 2 * j) % ranks) for i in range(ranks)])

    def home(part, j):
        return lax.ppermute(part, "dp", [(i, (i - 2 * j) % ranks) for i in range(ranks)])

    near = qkv_weight
    far = lax.ppermute(qkv_weight, "dp", [(i, i ^ 1) for i in range(ranks)])
    gain = norm_gain
    guests = []
    rows = tokens[0]
    for part in range(HALVES):
        sent = norm_sent(rows, gain, part, depth, chips)
        guests.append([away(piece, j) for j, piece in enumerate(sent, 1)])

    half = HD // 2
    places = (rank * tok + jnp.arange(tok, dtype=jnp.int32)).astype(jnp.float32)
    freqs = 500000.0 ** (-2.0 * jnp.arange(half, dtype=jnp.float32) / HD)
    angles = places[:, None] * freqs[None, :]
    cosine = jnp.cos(angles)
    sine = jnp.sin(angles)
    cosine = jnp.concatenate([cosine, cosine], axis=1)
    sine = jnp.concatenate([-sine, sine], axis=1)

    docs = doc_ids[0]
    spots = jnp.arange(tok, dtype=jnp.int32)
    allow = [(spots[None, :] <= spots[:, None]) & (docs[None, :] == docs[:, None])]
    for hop in range(1, hops + 1):
        other = lax.ppermute(doc_ids, "seq", [(i, i + hop) for i in range(count - hop)])[0]
        allow.append((rank >= hop) & (other[None, :] == docs[:, None]))
    bias = jnp.where(jnp.concatenate(allow, axis=1), 0.0, -1e30).astype(jnp.float32)

    rows, bias, cosine, sine = lax.optimization_barrier((rows, bias, cosine, sine))
    own = own_product(rows, gain, near, far)

    kv_got, q_got = [], []
    for part in range(HALVES):
        sent = [guest_product(piece, near, far, QW, 2 * KW) for piece in guests[part]]
        kv_got.append([home(piece, j) for j, piece in enumerate(sent, 1)])
        sent = [guest_product(piece, near, far, 0, QW) for piece in guests[part]]
        q_got.append([home(piece, j) for j, piece in enumerate(sent, 1)])
    chunks = []
    for part in range(HALVES):
        chunks.append(finish_kv(own, kv_got[part], cosine, sine, part))
    kv_blocks = list(chunks)
    for _ in range(hops):
        for part in range(HALVES):
            chunks[part] = lax.ppermute(chunks[part], "seq", [(i, i + 1) for i in range(count - 1)])
        kv_blocks += chunks

    result = None
    for part in range(HALVES):
        picks = []
        for p in range(len(kv_blocks)):
            start = -(p // HALVES) * tok + (p % HALVES) * step
            ahead = start > (part + 1) * step - 1
            behind = part * step - (start + step - 1) > reach
            if not (ahead or behind):
                picks.append(p)
        result = attend(
            own,
            q_got[part],
            [kv_blocks[p] for p in picks],
            picks,
            bias,
            cosine,
            sine,
            part,
            result,
        )
    return result[None]


def solution(mesh):
    in_specs = (P(("group", "dp"), "seq", None), P(), P("dp", None), P(("group", "dp"), "seq"))
    out_specs = P(("group", "dp"), "seq", None)
    return jax.shard_map(local, mesh=mesh, in_specs=in_specs, out_specs=out_specs, check_vma=False)
```

time: 297 us -> 110 us (0.37)
  waiting for transfers between devices: 189 us -> 26.7 us
  Pallas kernels: 0 us -> 53.7 us
  blocking collectives: 37.5 us -> 0 us
  matrix products: 20.9 us -> 0 us
  starting transfers between devices: 11.5 us -> 25.3 us
  local copies, waits for them, and re-layouts: 13.5 us -> 0 us
  between operations: 13.6 us -> 0.27 us
  other arithmetic: 10.1 us -> 3.35 us
    all_gather x1 -> x0, waiting for transfers between devices: 157 us -> none  [local(): lax.all_gather(qkv_weight, 'dp', axis=0, tiled=True)]
    pallas_call x0 -> x11, Pallas kernels: none -> 53.7 us  [the longest x4 20.4 us: guest_product(): pl.pallas_call(functools.partial(guest_kernel, first, tile), out_shape=ja...]
    all_to_all x3 -> x0, waiting for transfers between devices: 30.4 us -> none  [the longest x1 22.4 us: local(): lax.all_to_all(q_sent, 'seq', split_axis=1, concat_axis=0, tiled=True)]
    ppermute x0 -> x13, waiting for transfers between devices: none -> 26.7 us  [the longest x2 19.4 us: away(): lax.ppermute(part, 'dp', [(i, (i + 2 * j) % ranks) for i in range(ranks)])]
    all_to_all x1 -> x0, blocking collectives: 26.1 us -> none  [local(): return lax.all_to_all(back, 'seq', split_axis=0, concat_axis=2, tiled=True)]
    ppermute x0 -> x13, starting transfers between devices: none -> 25.3 us  [the longest x2 10 us: local(): lax.ppermute(doc_ids, 'seq', [(i, i + hop) for i in range(count - hop)])[0]]
    dot_general x5 -> x0, matrix products: 20.9 us -> none  [the longest x1 11.6 us: local(): jnp.dot(normed, lax.all_gather(qkv_weight, 'dp', axis=0, tiled=True), pre...]
    all_to_all x3 -> x0, starting transfers between devices: 11.5 us -> none  [the longest x1 4.59 us: local(): lax.all_to_all(values, 'seq', split_axis=1, concat_axis=0, tiled=True)]
  transfers between devices with their start and end apart: 4 -> 13, of which waited for: 3 -> 3; matrix products, arithmetic and copies ran while one was open for 2% -> 3% of each run, Pallas kernels for 0% -> 43%
where the time goes in v2:
time: 110 us; the launch traced here: 109 us
  Pallas kernels  53.7 us (49%)
  waiting for transfers between devices  26.7 us (24%)
  starting transfers between devices  25.3 us (23%)
  other arithmetic  3.35 us (3%)
    pallas_call x4, Pallas kernels, guest_product(): pl.pallas_call(functools.partial(guest_kernel, first, tile), out_shape=ja...  20.4 us
    ppermute x2, waiting for transfers between devices, away(): lax.ppermute(part, 'dp', [(i, (i + 2 * j) % ranks) for i in range(ranks)])  19.4 us
    pallas_call x2, Pallas kernels, attend(): pl.pallas_call(functools.partial(attend_kernel, len(got), picks), out_sha...  13 us
    ppermute x2, starting transfers between devices, local(): lax.ppermute(doc_ids, 'seq', [(i, i + hop) for i in range(count - hop)])[0]  10 us
    pallas_call x1, Pallas kernels, own_product(): pl.pallas_call(functools.partial(own_kernel, tile), out_shape=jax.ShapeDt...  9.58 us
    ppermute x4, starting transfers between devices, local(): lax.ppermute(chunks[part], 'seq', [(i, i + 1) for i in range(count - 1)])  8.45 us
    ppermute x4, waiting for transfers between devices, local(): lax.ppermute(chunks[part], 'seq', [(i, i + 1) for i in range(count - 1)])  7.2 us
    pallas_call x2, Pallas kernels, finish_kv(): pl.pallas_call(functools.partial(kv_kernel, len(got)), out_shape=jax.Shap...  5.85 us
  transfers between devices with their start and end apart: 13, of which 3 were waited for; matrix products, arithmetic and copies ran while one was open for 3% of the time, Pallas kernels for 43%

profile of v2, /device:TPU:0, one launch (start us, length us, event | category | flops | bytes accessed | tf_op | source)
XLA Modules:
  0.0 109.3 jit_solution(441708146482503959)
XLA Ops:
  0.0 0.5 collective-permute-start.2
  0.5 6.0 %collective-permute-start.1 = (s32[1,256]{1,0:T(1,128)}, s32[1,256]{1,0:T(1,128)}, u32[]{:S(2)}, u32[]{:S(2)}) collective-permute-start(s32[1,256]{1,0:T(1,128)} %param.7), channel_id=1, source_target_pairs={{0,2},{1,3},{4,6},{5,7},{8,10},{9,11},{12,14},{13,15},{16,18},{17,... | collective-permute-start | bytes 3080 | tf_op jit(solution)/shard_map/ppermute | solution.py:302
  6.5 4.0 %collective-permute-start = (s32[1,256]{1,0:T(1,128)}, s32[1,256]{1,0:T(1,128)}, u32[]{:S(2)}, u32[]{:S(2)}) collective-permute-start(s32[1,256]{1,0:T(1,128)} %param.7), channel_id=1, source_target_pairs={{0,1},{1,2},{2,3},{4,5},{5,6},{6,7},{8,9},{9,10},{10,11},{12,13},{... | collective-permute-start | bytes 3080 | tf_op jit(solution)/shard_map/ppermute | solution.py:302
  10.5 2.4 %norm_sent.2 = bf16[128,2048]{1,0:T(8,128)(2,1)} custom-call(bf16[256,4096]{1,0:T(8,128)(2,1)} %bitcast.5, bf16[4096]{0:T(1024)(128)(2,1)} %gain_ref.5), custom_call_target="tpu_custom_call" | custom-call | tf_op jit(solution)/shard_map/norm_sent/pallas_call | solution.py:49
  12.9 1.5 %collective-permute-start.3 = (bf16[128,2048]{1,0:T(8,128)(2,1)}, bf16[128,2048]{1,0:T(8,128)(2,1)}, u32[]{:S(2)}, u32[]{:S(2)}) collective-permute-start(bf16[128,2048]{1,0:T(8,128)(2,1)} %norm_sent.2), channel_id=1, source_target_pairs={{0,8},{4,12},{8,0},{12,4},{1,9},{5,13},{9,1},{13,5},{2,10},{6,14},... | collective-permute-start | bytes 1572872 | tf_op jit(solution)/shard_map/ppermute | solution.py:275
  14.4 2.4 %norm_sent.3 = bf16[128,2048]{1,0:T(8,128)(2,1)} custom-call(bf16[256,4096]{1,0:T(8,128)(2,1)} %bitcast.6, bf16[4096]{0:T(1024)(128)(2,1)} %gain_ref.5), custom_call_target="tpu_custom_call" | custom-call | tf_op jit(solution)/shard_map/norm_sent/pallas_call | solution.py:49
  16.9 0.5 collective-permute-start.5
  17.4 0.5 fusion.1
  17.9 0.9 pad_maximum_fusion
  18.8 19.4 %collective-permute-done.5.rows_hbm = bf16[128,2048]{1,0:T(8,128)(2,1)} collective-permute-done((bf16[128,2048]{1,0:T(8,128)(2,1)}, bf16[128,2048]{1,0:T(8,128)(2,1)}, u32[]{:S(2)}, u32[]{:S(2)}) %collective-permute-start.5) | collective-permute-done | bytes 524320 | tf_op jit(solution)/shard_map/ppermute | solution.py:275
  38.3 0.0 collective-permute-done.2.far_hbm
  38.3 3.8 %guest_product.5 = bf16[128,1024]{1,0:T(8,128)(2,1)} custom-call(bf16[128,2048]{1,0:T(8,128)(2,1)} %collective-permute-done.5.rows_hbm, bf16[1024,3072]{1,0:T(8,128)(2,1)} %near_hbm.9, bf16[1024,3072]{1,0:T(8,128)(2,1)} %collective-permute-done.2.far_hbm), custom_call_target="tpu_custom_call" | custom-call | tf_op jit(solution)/shard_map/guest_product/pallas_call | solution.py:131
  42.1 1.5 %collective-permute-start.6 = (bf16[128,1024]{1,0:T(8,128)(2,1)}, bf16[128,1024]{1,0:T(8,128)(2,1)}, u32[]{:S(2)}, u32[]{:S(2)}) collective-permute-start(bf16[128,1024]{1,0:T(8,128)(2,1)} %guest_product.5), channel_id=1, source_target_pairs={{0,8},{4,12},{8,0},{12,4},{1,9},{5,13},{9,1},{13,5},{2,10},{6,14},... | collective-permute-start | bytes 786440 | tf_op jit(solution)/shard_map/ppermute | solution.py:278
  43.7 3.8 %guest_product.6 = bf16[128,1024]{1,0:T(8,128)(2,1)} custom-call(bf16[128,2048]{1,0:T(8,128)(2,1)} %collective-permute-done.3.rows_hbm, bf16[1024,3072]{1,0:T(8,128)(2,1)} %near_hbm.9, bf16[1024,3072]{1,0:T(8,128)(2,1)} %collective-permute-done.2.far_hbm), custom_call_target="tpu_custom_call" | custom-call | tf_op jit(solution)/shard_map/guest_product/pallas_call | solution.py:131
  47.5 0.6 collective-permute-start.7
  48.1 1.0 fusion
  49.1 1.0 add_select_fusion.bias_ref
  50.0 6.4 %guest_product.7 = bf16[128,2048]{1,0:T(8,128)(2,1)} custom-call(bf16[128,2048]{1,0:T(8,128)(2,1)} %collective-permute-done.5.rows_hbm, bf16[1024,3072]{1,0:T(8,128)(2,1)} %near_hbm.9, bf16[1024,3072]{1,0:T(8,128)(2,1)} %collective-permute-done.2.far_hbm), custom_call_target="tpu_custom_call" | custom-call | tf_op jit(solution)/shard_map/guest_product/pallas_call | solution.py:131
  56.4 1.5 %collective-permute-start.11 = (bf16[128,2048]{1,0:T(8,128)(2,1)}, bf16[128,2048]{1,0:T(8,128)(2,1)}, u32[]{:S(2)}, u32[]{:S(2)}) collective-permute-start(bf16[128,2048]{1,0:T(8,128)(2,1)} %guest_product.7), channel_id=1, source_target_pairs={{0,8},{4,12},{8,0},{12,4},{1,9},{5,13},{9,1},{13,5},{2,10},{6,14},... | collective-permute-start | bytes 1572872 | tf_op jit(solution)/shard_map/ppermute | solution.py:278
  58.0 9.6 %own_product.1.own_ref = f32[256,3072]{1,0:T(8,128)} custom-call(bf16[256,4096]{1,0:T(8,128)(2,1)} %bitcast.7, bf16[4096]{0:T(1024)(128)(2,1)} %gain_ref.5, bf16[1024,3072]{1,0:T(8,128)(2,1)} %near_hbm.9, bf16[1024,3072]{1,0:T(8,128)(2,1)} %collective-permute-done.2.far_hbm), custom_call_target="tpu_custom_call" | custom-call | tf_op jit(solution)/shard_map/own_product/pallas_call | solution.py:103
  67.6 2.9 %finish_kv.2.refs_1_ = bf16[128,1024]{1,0:T(8,128)(2,1)} custom-call(f32[256,128]{1,0:T(8,128)} %get-tuple-element.9.cos_ref, f32[256,128]{1,0:T(8,128)} %get-tuple-element.10.sin_ref, f32[256,3072]{1,0:T(8,128)} %own_product.1.own_ref, bf16[128,1024]{1,0:T(8,128)(2,1)} %collective-permute-done.6.refs_0_), custom_call_target="tpu_custom_call" | custom-call | tf_op jit(solution)/shard_map/finish_kv/pallas_call | solution.py:180
  70.5 2.4 %collective-permute-start.8 = (bf16[128,1024]{1,0:T(8,128)(2,1)}, bf16[128,1024]{1,0:T(8,128)(2,1)}, u32[]{:S(2)}, u32[]{:S(2)}) collective-permute-start(bf16[128,1024]{1,0:T(8,128)(2,1)} %finish_kv.2.refs_1_), channel_id=1, source_target_pairs={{0,1},{1,2},{2,3},{4,5},{5,6},{6,7},{8,9},{9,10},{10,11},{12,13},{... | collective-permute-start | bytes 786440 | tf_op jit(solution)/shard_map/ppermute | solution.py:321
  72.9 2.9 %finish_kv.3.refs_2_ = bf16[128,1024]{1,0:T(8,128)(2,1)} custom-call(f32[256,128]{1,0:T(8,128)} %get-tuple-element.9.cos_ref, f32[256,128]{1,0:T(8,128)} %get-tuple-element.10.sin_ref, f32[256,3072]{1,0:T(8,128)} %own_product.1.own_ref, bf16[128,1024]{1,0:T(8,128)(2,1)} %collective-permute-done.7.refs_0_), custom_call_target="tpu_custom_call" | custom-call | tf_op jit(solution)/shard_map/finish_kv/pallas_call | solution.py:180
  75.9 2.0 %collective-permute-start.9 = (bf16[128,1024]{1,0:T(8,128)(2,1)}, bf16[128,1024]{1,0:T(8,128)(2,1)}, u32[]{:S(2)}, u32[]{:S(2)}) collective-permute-start(bf16[128,1024]{1,0:T(8,128)(2,1)} %finish_kv.3.refs_2_), channel_id=1, source_target_pairs={{0,1},{1,2},{2,3},{4,5},{5,6},{6,7},{8,9},{9,10},{10,11},{12,13},{... | collective-permute-start | bytes 786440 | tf_op jit(solution)/shard_map/ppermute | solution.py:321
  77.9 6.4 %guest_product.4 = bf16[128,2048]{1,0:T(8,128)(2,1)} custom-call(bf16[128,2048]{1,0:T(8,128)(2,1)} %collective-permute-done.3.rows_hbm, bf16[1024,3072]{1,0:T(8,128)(2,1)} %near_hbm.9, bf16[1024,3072]{1,0:T(8,128)(2,1)} %collective-permute-done.2.far_hbm), custom_call_target="tpu_custom_call" | custom-call | tf_op jit(solution)/shard_map/guest_product/pallas_call | solution.py:131
  84.2 0.6 collective-permute-start.4
  84.8 2.0 %collective-permute-start.12 = (bf16[128,1024]{1,0:T(8,128)(2,1)}, bf16[128,1024]{1,0:T(8,128)(2,1)}, u32[]{:S(2)}, u32[]{:S(2)}) collective-permute-start(bf16[128,1024]{1,0:T(8,128)(2,1)} %collective-permute-done.8.refs_2_.refs_3_), channel_id=1, source_target_pairs={{0,1},{1,2},{2,3},{4,5},{5,6},{6,7},{8,9},{9,10},{10,11},{12,13},{... | collective-permute-start | bytes 786440 | tf_op jit(solution)/shard_map/ppermute | solution.py:321
  86.9 2.0 %collective-permute-start.10 = (bf16[128,1024]{1,0:T(8,128)(2,1)}, bf16[128,1024]{1,0:T(8,128)(2,1)}, u32[]{:S(2)}, u32[]{:S(2)}) collective-permute-start(bf16[128,1024]{1,0:T(8,128)(2,1)} %collective-permute-done.9.refs_3_.refs_4_), channel_id=1, source_target_pairs={{0,1},{1,2},{2,3},{4,5},{5,6},{6,7},{8,9},{9,10},{10,11},{12,13},{... | collective-permute-start | bytes 786440 | tf_op jit(solution)/shard_map/ppermute | solution.py:321
  88.9 4.3 %collective-permute-done.12.refs_4_ = bf16[128,1024]{1,0:T(8,128)(2,1)} collective-permute-done((bf16[128,1024]{1,0:T(8,128)(2,1)}, bf16[128,1024]{1,0:T(8,128)(2,1)}, u32[]{:S(2)}, u32[]{:S(2)}) %collective-permute-start.12) | collective-permute-done | bytes 262176 | tf_op jit(solution)/shard_map/ppermute | solution.py:321
  93.2 2.9 %collective-permute-done.10.refs_5_ = bf16[128,1024]{1,0:T(8,128)(2,1)} collective-permute-done((bf16[128,1024]{1,0:T(8,128)(2,1)}, bf16[128,1024]{1,0:T(8,128)(2,1)}, u32[]{:S(2)}, u32[]{:S(2)}) %collective-permute-start.10) | collective-permute-done | bytes 262176 | tf_op jit(solution)/shard_map/ppermute | solution.py:321
  96.1 6.5 %attend.2.refs_6_ = bf16[256,2048]{1,0:T(8,128)(2,1)} custom-call(f32[256,128]{1,0:T(8,128)} %get-tuple-element.9.cos_ref, f32[256,128]{1,0:T(8,128)} %get-tuple-element.10.sin_ref, f32[256,768]{1,0:T(8,128)} %add_select_fusion.bias_ref, f32[256,3072]{1,0:T(8,128)} %own_product.1.own_ref, bf16[128,2048]{1,0:T(8,128)(2,1)} %collective-permute-done.11.refs_0_, ...), custom_call_target="tpu_custom_call" | custom-call | tf_op jit(solution)/shard_map/attend/pallas_call | solution.py:246
  102.6 6.5 %attend.3 = bf16[256,2048]{1,0:T(8,128)(2,1)} custom-call(f32[256,128]{1,0:T(8,128)} %get-tuple-element.9.cos_ref, f32[256,128]{1,0:T(8,128)} %get-tuple-element.10.sin_ref, f32[256,768]{1,0:T(8,128)} %add_select_fusion.bias_ref, f32[256,3072]{1,0:T(8,128)} %own_product.1.own_ref, ...), custom_call_target="tpu_custom_call", output_to_operand_aliasing={{}: (10, {})} | custom-call | tf_op jit(solution)/shard_map/attend/pallas_call | solution.py:246
  (11 shorter events, 0.0 us)
Async XLA Ops:
  0.0 38.3 %collective-permute-start.2 = (bf16[1024,3072]{1,0:T(8,128)(2,1)}, bf16[1024,3072]{1,0:T(8,128)(2,1)}, u32[]{:S(2)}, u32[]{:S(2)}) collective-permute-start(bf16[1024,3072]{1,0:T(8,128)(2,1)} %near_hbm.9), channel_id=1, source_target_pairs={{0,4},{4,0},{8,12},{12,8},{1,5},{5,1},{9,13},{13,9},{2,6},{6,2},{1... | collective-permute-start | bytes 18874376 | tf_op jit(solution)/shard_map/ppermute | solution.py:281
  0.5 47.6 %collective-permute-start.1 = (s32[1,256]{1,0:T(1,128)}, s32[1,256]{1,0:T(1,128)}, u32[]{:S(2)}, u32[]{:S(2)}) collective-permute-start(s32[1,256]{1,0:T(1,128)} %param.7), channel_id=1, source_target_pairs={{0,2},{1,3},{4,6},{5,7},{8,10},{9,11},{12,14},{13,15},{16,18},{17,... | collective-permute-start | bytes 3080 | tf_op jit(solution)/shard_map/ppermute | solution.py:302
  6.5 41.6 %collective-permute-start = (s32[1,256]{1,0:T(1,128)}, s32[1,256]{1,0:T(1,128)}, u32[]{:S(2)}, u32[]{:S(2)}) collective-permute-start(s32[1,256]{1,0:T(1,128)} %param.7), channel_id=1, source_target_pairs={{0,1},{1,2},{2,3},{4,5},{5,6},{6,7},{8,9},{9,10},{10,11},{12,13},{... | collective-permute-start | bytes 3080 | tf_op jit(solution)/shard_map/ppermute | solution.py:302
  12.9 30.7 %collective-permute-start.3 = (bf16[128,2048]{1,0:T(8,128)(2,1)}, bf16[128,2048]{1,0:T(8,128)(2,1)}, u32[]{:S(2)}, u32[]{:S(2)}) collective-permute-start(bf16[128,2048]{1,0:T(8,128)(2,1)} %norm_sent.2), channel_id=1, source_target_pairs={{0,8},{4,12},{8,0},{12,4},{1,9},{5,13},{9,1},{13,5},{2,10},{6,14},... | collective-permute-start | bytes 1572872 | tf_op jit(solution)/shard_map/ppermute | solution.py:275
  16.9 21.4 %collective-permute-start.5 = (bf16[128,2048]{1,0:T(8,128)(2,1)}, bf16[128,2048]{1,0:T(8,128)(2,1)}, u32[]{:S(2)}, u32[]{:S(2)}) collective-permute-start(bf16[128,2048]{1,0:T(8,128)(2,1)} %norm_sent.3), channel_id=1, source_target_pairs={{0,8},{4,12},{8,0},{12,4},{1,9},{5,13},{9,1},{13,5},{2,10},{6,14},... | collective-permute-start | bytes 1572872 | tf_op jit(solution)/shard_map/ppermute | solution.py:275
  42.1 25.4 %collective-permute-start.6 = (bf16[128,1024]{1,0:T(8,128)(2,1)}, bf16[128,1024]{1,0:T(8,128)(2,1)}, u32[]{:S(2)}, u32[]{:S(2)}) collective-permute-start(bf16[128,1024]{1,0:T(8,128)(2,1)} %guest_product.5), channel_id=1, source_target_pairs={{0,8},{4,12},{8,0},{12,4},{1,9},{5,13},{9,1},{13,5},{2,10},{6,14},... | collective-permute-start | bytes 786440 | tf_op jit(solution)/shard_map/ppermute | solution.py:278
  47.5 25.4 %collective-permute-start.7 = (bf16[128,1024]{1,0:T(8,128)(2,1)}, bf16[128,1024]{1,0:T(8,128)(2,1)}, u32[]{:S(2)}, u32[]{:S(2)}) collective-permute-start(bf16[128,1024]{1,0:T(8,128)(2,1)} %guest_product.6), channel_id=1, source_target_pairs={{0,8},{4,12},{8,0},{12,4},{1,9},{5,13},{9,1},{13,5},{2,10},{6,14},... | collective-permute-start | bytes 786440 | tf_op jit(solution)/shard_map/ppermute | solution.py:278
  56.4 32.4 %collective-permute-start.11 = (bf16[128,2048]{1,0:T(8,128)(2,1)}, bf16[128,2048]{1,0:T(8,128)(2,1)}, u32[]{:S(2)}, u32[]{:S(2)}) collective-permute-start(bf16[128,2048]{1,0:T(8,128)(2,1)} %guest_product.7), channel_id=1, source_target_pairs={{0,8},{4,12},{8,0},{12,4},{1,9},{5,13},{9,1},{13,5},{2,10},{6,14},... | collective-permute-start | bytes 1572872 | tf_op jit(solution)/shard_map/ppermute | solution.py:278
  70.5 14.4 %collective-permute-start.8 = (bf16[128,1024]{1,0:T(8,128)(2,1)}, bf16[128,1024]{1,0:T(8,128)(2,1)}, u32[]{:S(2)}, u32[]{:S(2)}) collective-permute-start(bf16[128,1024]{1,0:T(8,128)(2,1)} %finish_kv.2.refs_1_), channel_id=1, source_target_pairs={{0,1},{1,2},{2,3},{4,5},{5,6},{6,7},{8,9},{9,10},{10,11},{12,13},{... | collective-permute-start | bytes 786440 | tf_op jit(solution)/shard_map/ppermute | solution.py:321
  75.9 11.0 %collective-permute-start.9 = (bf16[128,1024]{1,0:T(8,128)(2,1)}, bf16[128,1024]{1,0:T(8,128)(2,1)}, u32[]{:S(2)}, u32[]{:S(2)}) collective-permute-start(bf16[128,1024]{1,0:T(8,128)(2,1)} %finish_kv.3.refs_2_), channel_id=1, source_target_pairs={{0,1},{1,2},{2,3},{4,5},{5,6},{6,7},{8,9},{9,10},{10,11},{12,13},{... | collective-permute-start | bytes 786440 | tf_op jit(solution)/shard_map/ppermute | solution.py:321
  84.2 18.3 %collective-permute-start.4 = (bf16[128,2048]{1,0:T(8,128)(2,1)}, bf16[128,2048]{1,0:T(8,128)(2,1)}, u32[]{:S(2)}, u32[]{:S(2)}) collective-permute-start(bf16[128,2048]{1,0:T(8,128)(2,1)} %guest_product.4), channel_id=1, source_target_pairs={{0,8},{4,12},{8,0},{12,4},{1,9},{5,13},{9,1},{13,5},{2,10},{6,14},... | collective-permute-start | bytes 1572872 | tf_op jit(solution)/shard_map/ppermute | solution.py:278
  84.8 8.3 %collective-permute-start.12 = (bf16[128,1024]{1,0:T(8,128)(2,1)}, bf16[128,1024]{1,0:T(8,128)(2,1)}, u32[]{:S(2)}, u32[]{:S(2)}) collective-permute-start(bf16[128,1024]{1,0:T(8,128)(2,1)} %collective-permute-done.8.refs_2_.refs_3_), channel_id=1, source_target_pairs={{0,1},{1,2},{2,3},{4,5},{5,6},{6,7},{8,9},{9,10},{10,11},{12,13},{... | collective-permute-start | bytes 786440 | tf_op jit(solution)/shard_map/ppermute | solution.py:321
  86.9 9.2 %collective-permute-start.10 = (bf16[128,1024]{1,0:T(8,128)(2,1)}, bf16[128,1024]{1,0:T(8,128)(2,1)}, u32[]{:S(2)}, u32[]{:S(2)}) collective-permute-start(bf16[128,1024]{1,0:T(8,128)(2,1)} %collective-permute-done.9.refs_3_.refs_4_), channel_id=1, source_target_pairs={{0,1},{1,2},{2,3},{4,5},{5,6},{6,7},{8,9},{9,10},{10,11},{12,13},{... | collective-permute-start | bytes 786440 | tf_op jit(solution)/shard_map/ppermute | solution.py:321

commit v3 on v2

v3 whole, which is shorter than its diff:
```python
import functools
import math

import jax
import jax.numpy as jnp
from jax import lax
from jax.experimental import pallas as pl
from jax.experimental.pallas import tpu as pltpu
from jax.sharding import PartitionSpec as P


HD = 128
QH = 16
KVH = 4
QW = 2048
KW = 512
SHARE = QH // KVH
EXP2_SCALE = math.log2(math.e) / math.sqrt(HD)
HALVES = 2

ANY = pl.BlockSpec(memory_space=pl.ANY)
VMEM = pl.BlockSpec(memory_space=pltpu.VMEM)
PARAMS = pltpu.CompilerParams(vmem_limit_bytes=20 * 1024 * 1024)


def row_scale(values):
    return lax.rsqrt(jnp.mean(values * values, axis=-1, keepdims=True) + 1e-05)


def write_blocks(tok_ref, gain_ref, scale, out_ref, chip, core):
    depth = out_ref.shape[1] // 2
    for half in range(2):
        block = 2 * chip + (core if half == 0 else 1 - core)
        cut = pl.ds(pl.multiple_of(block * depth, 128), depth)
        piece = tok_ref[:, cut].astype(jnp.float32) * scale
        piece = piece * gain_ref[cut].astype(jnp.float32)[None, :]
        out_ref[:, half * depth : (half + 1) * depth] = piece.astype(jnp.bfloat16)


def norm_kernel(chips, part, tok_ref, gain_ref, *out_refs):
    place = lax.axis_index("dp")
    step = out_refs[0].shape[0]
    tok_ref = tok_ref.at[pl.ds(part * step, step)]
    scale = row_scale(tok_ref[...].astype(jnp.float32))
    for j, out_ref in enumerate(out_refs, 1):
        chip = lax.rem(lax.div(place, 2) + j, chips)
        write_blocks(tok_ref, gain_ref, scale, out_ref, chip, lax.rem(place, 2))


def norm_sent(rows, gain, part, depth, chips):
    step = rows.shape[0] // HALVES
    return pl.pallas_call(
        functools.partial(norm_kernel, chips, part),
        out_shape=[jax.ShapeDtypeStruct((step, 2 * depth), jnp.bfloat16)] * (chips - 1),
        in_specs=[VMEM, VMEM],
        out_specs=[VMEM] * (chips - 1),
        compiler_params=PARAMS,
        name="norm_sent",
    )(rows, gain)


def multiply(rows, near, far, first, out_ref, tile=512):
    depth = near.shape[0]
    for start in range(0, out_ref.shape[1], tile):
        cut = slice(first + start, first + start + tile)
        total = jnp.dot(rows[:, :depth], near[:, cut], preferred_element_type=jnp.float32)
        total += jnp.dot(rows[:, depth:], far[:, cut], preferred_element_type=jnp.float32)
        out_ref[:, start : start + tile] = total.astype(out_ref.dtype)


def own_kernel(tok_ref, gain_ref, near, far, out_ref, mine):
    place = lax.axis_index("dp")
    scale = row_scale(tok_ref[...].astype(jnp.float32))
    write_blocks(tok_ref, gain_ref, scale, mine, lax.div(place, 2), lax.rem(place, 2))
    multiply(mine, near, far, 0, out_ref)


def own_product(rows, gain, near, far):
    tok = rows.shape[0]
    depth, columns = near.shape
    return pl.pallas_call(
        own_kernel,
        out_shape=jax.ShapeDtypeStruct((tok, columns), jnp.float32),
        in_specs=[VMEM] * 4,
        out_specs=VMEM,
        scratch_shapes=[pltpu.VMEM((tok, 2 * depth), jnp.bfloat16)],
        compiler_params=PARAMS,
        name="own_product",
    )(rows, gain, near, far)


def guest_kernel(first, rows, near, far, out_ref):
    multiply(rows, near, far, first, out_ref)


def guest_product(rows, near, far, first, width):
    return pl.pallas_call(
        functools.partial(guest_kernel, first),
        out_shape=jax.ShapeDtypeStruct((rows.shape[0], width), jnp.bfloat16),
        in_specs=[VMEM] * 3,
        out_specs=VMEM,
        compiler_params=PARAMS,
        name="guest_product",
    )(rows, near, far)


def turn(head, cosine, sine):
    return head * cosine + pltpu.roll(head, HD // 2, 1) * sine


def kv_kernel(part, cos_ref, sin_ref, own_ref, *refs):
    *got_refs, out_ref = refs
    step = out_ref.shape[0]
    rows = slice(part * step, (part + 1) * step)
    cosine, sine = cos_ref[rows], sin_ref[rows]
    for start in range(0, 2 * KW, HD):
        cut = slice(start, start + HD)
        total = own_ref[rows, QW + start : QW + start + HD]
        for got_ref in got_refs:
            total += got_ref[:, cut].astype(jnp.float32)
        if start < KW:
            total = turn(total, cosine, sine)
        out_ref[:, cut] = total.astype(jnp.bfloat16)


def finish_kv(own, got, cosine, sine, part):
    return pl.pallas_call(
        functools.partial(kv_kernel, part),
        out_shape=jax.ShapeDtypeStruct(got[0].shape, jnp.bfloat16),
        in_specs=[VMEM] * (3 + len(got)),
        out_specs=VMEM,
        compiler_params=PARAMS,
        name="finish_kv",
    )(cosine, sine, own, *got)


def attend_kernel(part, parts, picks, cos_ref, sin_ref, bias_ref, own_ref, *refs):
    blocks = len(picks)
    got_refs = refs[:parts]
    kv_refs = refs[parts : parts + blocks]
    out_hbm, out, sems = refs[-3:]
    step = out.shape[0]
    rows = slice(part * step, (part + 1) * step)
    cosine, sine = cos_ref[rows], sin_ref[rows]
    bias = jnp.concatenate([bias_ref[rows, p * step : (p + 1) * step] for p in picks], axis=1)
    copies = []
    for group in range(KVH):
        start = group * HD
        keys = jnp.concatenate([ref[:, start : start + HD] for ref in kv_refs], axis=0)
        start += KW
        values = jnp.concatenate([ref[:, start : start + HD] for ref in kv_refs], axis=0)
        values = jnp.concatenate([values, jnp.ones_like(values)], axis=1)
        for head in range(group * SHARE, (group + 1) * SHARE):
            cut = slice(head * HD, (head + 1) * HD)
            query = own_ref[rows, cut]
            for got_ref in got_refs:
                query += got_ref[:, cut].astype(jnp.float32)
            query = turn(query, cosine, sine).astype(jnp.bfloat16)
            scores = lax.dot_general(
                query, keys, (((1,), (1,)), ((), ())), preferred_element_type=jnp.float32
            )
            scores = scores + bias
            peak = jnp.max(scores, axis=-1, keepdims=True)
            expo = jnp.exp2((scores - peak) * EXP2_SCALE).astype(jnp.bfloat16)
            sums = jnp.dot(expo, values, preferred_element_type=jnp.float32)
            out[:, cut] = (sums[:, :HD] / sums[:, HD:]).astype(jnp.bfloat16)
        cut = pl.ds(group * SHARE * HD, SHARE * HD)
        copy = pltpu.make_async_copy(
            out.at[:, cut], out_hbm.at[pl.ds(part * step, step), cut], sems.at[group]
        )
        copy.start()
        copies.append(copy)
    for copy in copies:
        copy.wait()


def attend(own, got, kv_blocks, picks, bias, cosine, sine, part, previous):
    tok = own.shape[0]
    step = tok // HALVES
    operands = [cosine, sine, bias, own, *got, *kv_blocks]
    in_specs = [VMEM] * len(operands)
    aliases = {}
    if previous is not None:
        aliases = {len(operands): 0}
        operands.append(previous)
        in_specs.append(ANY)
    return pl.pallas_call(
        functools.partial(attend_kernel, part, len(got), picks),
        out_shape=jax.ShapeDtypeStruct((tok, QW), jnp.bfloat16),
        in_specs=in_specs,
        out_specs=ANY,
        scratch_shapes=[
            pltpu.VMEM((step, QW), jnp.bfloat16),
            pltpu.SemaphoreType.DMA((KVH,)),
        ],
        input_output_aliases=aliases,
        compiler_params=PARAMS,
        name="attend",
    )(*operands)


def local(tokens, norm_gain, qkv_weight, doc_ids):
    count = lax.axis_size("seq")
    rank = lax.axis_index("seq")
    ranks = lax.axis_size("dp")
    chips = ranks // 2
    tok = tokens.shape[1]
    depth = qkv_weight.shape[0]
    step = tok // HALVES
    reach = tok * count // 2 - 1
    hops = -(-reach // tok)

    def away(part, j):
        return lax.ppermute(part, "dp", [(i, (i + 2 * j) % ranks) for i in range(ranks)])

    def home(part, j):
        return lax.ppermute(part, "dp", [(i, (i - 2 * j) % ranks) for i in range(ranks)])

    near = qkv_weight
    far = lax.ppermute(qkv_weight, "dp", [(i, i ^ 1) for i in range(ranks)])
    gain = norm_gain
    guests = []
    rows = tokens[0]
    for part in range(HALVES):
        sent = norm_sent(rows, gain, part, depth, chips)
        guests.append([away(piece, j) for j, piece in enumerate(sent, 1)])

    half = HD // 2
    places = (rank * tok + jnp.arange(tok, dtype=jnp.int32)).astype(jnp.float32)
    freqs = 500000.0 ** (-2.0 * jnp.arange(half, dtype=jnp.float32) / HD)
    angles = places[:, None] * freqs[None, :]
    cosine = jnp.cos(angles)
    sine = jnp.sin(angles)
    cosine = jnp.concatenate([cosine, cosine], axis=1)
    sine = jnp.concatenate([-sine, sine], axis=1)

    docs = doc_ids[0]
    spots = jnp.arange(tok, dtype=jnp.int32)
    allow = [(spots[None, :] <= spots[:, None]) & (docs[None, :] == docs[:, None])]
    for hop in range(1, hops + 1):
        other = lax.ppermute(doc_ids, "seq", [(i, i + hop) for i in range(count - hop)])[0]
        allow.append((rank >= hop) & (other[None, :] == docs[:, None]))
    bias = jnp.where(jnp.concatenate(allow, axis=1), 0.0, -1e30).astype(jnp.float32)

    guests[1], bias, cosine, sine = lax.optimization_barrier((guests[1], bias, cosine, sine))
    own = own_product(rows, gain, near, far)

    kv_got, q_got = [], []
    for part in range(HALVES):
        sent = [guest_product(piece, near, far, QW, 2 * KW) for piece in guests[part]]
        kv_got.append([home(piece, j) for j, piece in enumerate(sent, 1)])
        sent = [guest_product(piece, near, far, 0, QW) for piece in guests[part]]
        q_got.append([home(piece, j) for j, piece in enumerate(sent, 1)])
    chunks = []
    for part in range(HALVES):
        chunks.append(finish_kv(own, kv_got[part], cosine, sine, part))
    kv_blocks = list(chunks)
    for _ in range(hops):
        for part in range(HALVES):
            chunks[part] = lax.ppermute(chunks[part], "seq", [(i, i + 1) for i in range(count - 1)])
        kv_blocks += chunks

    result = None
    for part in range(HALVES):
        picks = []
        for p in range(len(kv_blocks)):
            start = -(p // HALVES) * tok + (p % HALVES) * step
            ahead = start > (part + 1) * step - 1
            behind = part * step - (start + step - 1) > reach
            if not (ahead or behind):
                picks.append(p)
        result = attend(
            own,
            q_got[part],
            [kv_blocks[p] for p in picks],
            picks,
            bias,
            cosine,
            sine,
            part,
            result,
        )
    return result[None]


def solution(mesh):
    in_specs = (P(("group", "dp"), "seq", None), P(), P("dp", None), P(("group", "dp"), "seq"))
    out_specs = P(("group", "dp"), "seq", None)
    return jax.shard_map(local, mesh=mesh, in_specs=in_specs, out_specs=out_specs, check_vma=False)
```

time: 110 us -> 93.3 us (0.85)
  Pallas kernels: 53.7 us -> 31 us
  local copies, waits for them, and re-layouts: 0 us -> 5.1 us
  starting transfers between devices: 25.3 us -> 28.8 us
  other arithmetic: 3.35 us -> 0.96 us
    pallas_call x11, Pallas kernels: 53.7 us -> 31 us  [the longest x4 15.5 us: guest_product(): pl.pallas_call(functools.partial(guest_kernel, first), out_shape=jax.Shap...]
    unnamed x0 -> x16, local copies, waits for them, and re-layouts: none -> 5.1 us
    ppermute x4, starting transfers between devices: 8.45 us -> 12.7 us  [local(): lax.ppermute(chunks[part], 'seq', [(i, i + 1) for i in range(count - 1)])]
    ppermute x4, waiting for transfers between devices: 7.2 us -> 5.31 us  [local(): lax.ppermute(chunks[part], 'seq', [(i, i + 1) for i in range(count - 1)])]
    ppermute x2, waiting for transfers between devices: 19.4 us -> 21.3 us  [away(): lax.ppermute(part, 'dp', [(i, (i + 2 * j) % ranks) for i in range(ranks)])]
  transfers between devices with their start and end apart: 13 -> 13, of which waited for: 3 -> 4; matrix products, arithmetic and copies ran while one was open for 3% -> 1% of each run, Pallas kernels for 43% -> 29%
where the time goes in v3:
time: 93.3 us; the launch traced here: 92.9 us
  Pallas kernels  31 us (33%)
  starting transfers between devices  28.8 us (31%)
  waiting for transfers between devices  26.7 us (29%)
  local copies, waits for them, and re-layouts  5.1 us (5%)
  other arithmetic  0.96 us (1%)
    ppermute x2, waiting for transfers between devices, away(): lax.ppermute(part, 'dp', [(i, (i + 2 * j) % ranks) for i in range(ranks)])  21.3 us
    pallas_call x4, Pallas kernels, guest_product(): pl.pallas_call(functools.partial(guest_kernel, first), out_shape=jax.Shap...  15.5 us
    ppermute x4, starting transfers between devices, local(): lax.ppermute(chunks[part], 'seq', [(i, i + 1) for i in range(count - 1)])  12.7 us
    ppermute x2, starting transfers between devices, local(): lax.ppermute(doc_ids, 'seq', [(i, i + hop) for i in range(count - hop)])[0]  9.09 us
    pallas_call x2, Pallas kernels, attend(): pl.pallas_call(functools.partial(attend_kernel, part, len(got), picks), o...  7.59 us
    pallas_call x1, Pallas kernels, own_product(): pl.pallas_call(own_kernel, out_shape=jax.ShapeDtypeStruct((tok, columns),...  6.71 us
    ppermute x4, waiting for transfers between devices, local(): lax.ppermute(chunks[part], 'seq', [(i, i + 1) for i in range(count - 1)])  5.31 us
    unnamed x16, local copies, waits for them, and re-layouts  5.1 us
  transfers between devices with their start and end apart: 13, of which 4 were waited for; matrix products, arithmetic and copies ran while one was open for 1% of the time, Pallas kernels for 29%

profile of v3, /device:TPU:0, one launch (start us, length us, event | category | flops | bytes accessed | tf_op | source)
XLA Modules:
  0.0 92.9 jit_solution(1805238070774850434)
XLA Ops:
  0.0 0.5 collective-permute-start.3
  0.5 5.6 %collective-permute-start.2 = (s32[1,256]{1,0:T(1,128)}, s32[1,256]{1,0:T(1,128)S(1)}, u32[]{:S(2)}, u32[]{:S(2)}) collective-permute-start(s32[1,256]{1,0:T(1,128)} %param.7), channel_id=1, source_target_pairs={{0,2},{1,3},{4,6},{5,7},{8,10},{9,11},{12,14},{13,15},{16,18},{17,... | collective-permute-start | bytes 3080 | tf_op jit(solution)/shard_map/ppermute | solution.py:241
  6.1 3.5 %collective-permute-start.1 = (s32[1,256]{1,0:T(1,128)}, s32[1,256]{1,0:T(1,128)S(1)}, u32[]{:S(2)}, u32[]{:S(2)}) collective-permute-start(s32[1,256]{1,0:T(1,128)} %param.7), channel_id=1, source_target_pairs={{0,1},{1,2},{2,3},{4,5},{5,6},{6,7},{8,9},{9,10},{10,11},{12,13},{... | collective-permute-start | bytes 3080 | tf_op jit(solution)/shard_map/ppermute | solution.py:241
  9.6 1.6 %copy-done.1 = bf16[1,256,4096]{2,1,0:T(8,128)(2,1)S(1)} copy-done((bf16[1,256,4096]{2,1,0:T(8,128)(2,1)S(1)}, bf16[1,256,4096]{2,1,0:T(8,128)(2,1)}, u32[]{:S(2)}) %copy-start.1) | copy-done | bytes 2097176
  11.2 0.7 copy-done.3
  11.9 0.4 norm_sent.2
  12.3 1.6 %collective-permute-start = (bf16[128,2048]{1,0:T(8,128)(2,1)S(1)}, bf16[128,2048]{1,0:T(8,128)(2,1)S(1)}, u32[]{:S(2)}, u32[]{:S(2)}) collective-permute-start(bf16[128,2048]{1,0:T(8,128)(2,1)S(1)} %norm_sent.2), channel_id=1, source_target_pairs={{0,8},{4,12},{8,0},{12,4},{1,9},{5,13},{9,1},{13,5},{2,10},{6,14},... | collective-permute-start | bytes 1572872 | tf_op jit(solution)/shard_map/ppermute | solution.py:214
  13.9 0.4 norm_sent.3
  14.3 0.6 collective-permute-start.5
  14.9 0.5 fusion.1
  15.6 0.2 fusion
  15.9 21.3 %collective-permute-done.5.rows = bf16[128,2048]{1,0:T(8,128)(2,1)S(1)} collective-permute-done((bf16[128,2048]{1,0:T(8,128)(2,1)S(1)}, bf16[128,2048]{1,0:T(8,128)(2,1)S(1)}, u32[]{:S(2)}, u32[]{:S(2)}) %collective-permute-start.5) | collective-permute-done | bytes 524320 | tf_op jit(solution)/shard_map/ppermute | solution.py:214
  37.3 2.8 %copy-done = bf16[1024,3072]{1,0:T(8,128)(2,1)S(1)} copy-done((bf16[1024,3072]{1,0:T(8,128)(2,1)S(1)}, bf16[1024,3072]{1,0:T(8,128)(2,1)}, u32[]{:S(2)}) %copy-start) | copy-done | bytes 6291480
  40.0 3.5 %guest_product.5 = bf16[128,1024]{1,0:T(8,128)(2,1)S(1)} custom-call(bf16[128,2048]{1,0:T(8,128)(2,1)S(1)} %collective-permute-done.5.rows, bf16[1024,3072]{1,0:T(8,128)(2,1)S(1)} %copy-done, bf16[1024,3072]{1,0:T(8,128)(2,1)} %collective-permute-done.3.far), custom_call_target="tpu_custom_call" | custom-call | tf_op jit(solution)/shard_map/guest_product/pallas_call | solution.py:97
  43.5 1.6 %collective-permute-start.6 = (bf16[128,1024]{1,0:T(8,128)(2,1)S(1)}, bf16[128,1024]{1,0:T(8,128)(2,1)S(1)}, u32[]{:S(2)}, u32[]{:S(2)}) collective-permute-start(bf16[128,1024]{1,0:T(8,128)(2,1)S(1)} %guest_product.5), channel_id=1, source_target_pairs={{0,8},{4,12},{8,0},{12,4},{1,9},{5,13},{9,1},{13,5},{2,10},{6,14},... | collective-permute-start | bytes 786440 | tf_op jit(solution)/shard_map/ppermute | solution.py:217
  45.1 3.7 %guest_product.6 = bf16[128,1024]{1,0:T(8,128)(2,1)S(1)} custom-call(bf16[128,2048]{1,0:T(8,128)(2,1)S(1)} %collective-permute-done.rows, bf16[1024,3072]{1,0:T(8,128)(2,1)S(1)} %copy-done, bf16[1024,3072]{1,0:T(8,128)(2,1)} %collective-permute-done.3.far), custom_call_target="tpu_custom_call" | custom-call | tf_op jit(solution)/shard_map/guest_product/pallas_call | solution.py:97
  48.8 0.6 collective-permute-start.7
  49.4 4.3 %guest_product.7 = bf16[128,2048]{1,0:T(8,128)(2,1)S(1)} custom-call(bf16[128,2048]{1,0:T(8,128)(2,1)S(1)} %collective-permute-done.5.rows, bf16[1024,3072]{1,0:T(8,128)(2,1)S(1)} %copy-done, bf16[1024,3072]{1,0:T(8,128)(2,1)} %collective-permute-done.3.far), custom_call_target="tpu_custom_call" | custom-call | tf_op jit(solution)/shard_map/guest_product/pallas_call | solution.py:97
  53.7 1.3 %collective-permute-start.11 = (bf16[128,2048]{1,0:T(8,128)(2,1)S(1)}, bf16[128,2048]{1,0:T(8,128)(2,1)S(1)}, u32[]{:S(2)}, u32[]{:S(2)}) collective-permute-start(bf16[128,2048]{1,0:T(8,128)(2,1)S(1)} %guest_product.7), channel_id=1, source_target_pairs={{0,8},{4,12},{8,0},{12,4},{1,9},{5,13},{9,1},{13,5},{2,10},{6,14},... | collective-permute-start | bytes 1572872 | tf_op jit(solution)/shard_map/ppermute | solution.py:217
  55.0 6.7 %own_product.1.own_ref = f32[256,3072]{1,0:T(8,128)S(1)} custom-call(bf16[256,4096]{1,0:T(8,128)(2,1)S(1)} %bitcast.9, bf16[4096]{0:T(1024)(128)(2,1)S(1)} %copy-done.4, bf16[1024,3072]{1,0:T(8,128)(2,1)S(1)} %bitcast.6, bf16[1024,3072]{1,0:T(8,128)(2,1)} %collective-permute-done.3.far), custom_call_target="tpu_custom_call" | custom-call | tf_op jit(solution)/shard_map/own_product/pallas_call | solution.py:81
  61.8 0.2 finish_kv.2.refs_1_
  61.9 2.2 %collective-permute-start.8 = (bf16[128,1024]{1,0:T(8,128)(2,1)S(1)}, bf16[128,1024]{1,0:T(8,128)(2,1)S(1)}, u32[]{:S(2)}, u32[]{:S(2)}) collective-permute-start(bf16[128,1024]{1,0:T(8,128)(2,1)S(1)} %finish_kv.2.refs_1_), channel_id=1, source_target_pairs={{0,1},{1,2},{2,3},{4,5},{5,6},{6,7},{8,9},{9,10},{10,11},{12,13},{... | collective-permute-start | bytes 786440 | tf_op jit(solution)/shard_map/ppermute | solution.py:260
  64.3 1.9 %collective-permute-start.9 = (bf16[128,1024]{1,0:T(8,128)(2,1)S(1)}, bf16[128,1024]{1,0:T(8,128)(2,1)S(1)}, u32[]{:S(2)}, u32[]{:S(2)}) collective-permute-start(bf16[128,1024]{1,0:T(8,128)(2,1)S(1)} %finish_kv.3.refs_2_), channel_id=1, source_target_pairs={{0,1},{1,2},{2,3},{4,5},{5,6},{6,7},{8,9},{9,10},{10,11},{12,13},{... | collective-permute-start | bytes 786440 | tf_op jit(solution)/shard_map/ppermute | solution.py:260
  66.3 4.1 %guest_product.4 = bf16[128,2048]{1,0:T(8,128)(2,1)S(1)} custom-call(bf16[128,2048]{1,0:T(8,128)(2,1)S(1)} %collective-permute-done.rows, bf16[1024,3072]{1,0:T(8,128)(2,1)S(1)} %bitcast.6, bf16[1024,3072]{1,0:T(8,128)(2,1)} %collective-permute-done.3.far), custom_call_target="tpu_custom_call" | custom-call | tf_op jit(solution)/shard_map/guest_product/pallas_call | solution.py:97
  70.3 0.9 collective-permute-start.4
  71.2 4.0 %collective-permute-start.12 = (bf16[128,1024]{1,0:T(8,128)(2,1)S(1)}, bf16[128,1024]{1,0:T(8,128)(2,1)S(1)}, u32[]{:S(2)}, u32[]{:S(2)}) collective-permute-start(bf16[128,1024]{1,0:T(8,128)(2,1)S(1)} %collective-permute-done.8.refs_2_.refs_3_), channel_id=1, source_target_pairs={{0,1},{1,2},{2,3},{4,5},{5,6},{6,7},{8,9},{9,10},{10,11},{12,13},{... | collective-permute-start | bytes 786440 | tf_op jit(solution)/shard_map/ppermute | solution.py:260
  75.2 1.2 %collective-permute-done.9.refs_3_.refs_4_ = bf16[128,1024]{1,0:T(8,128)(2,1)S(1)} collective-permute-done((bf16[128,1024]{1,0:T(8,128)(2,1)S(1)}, bf16[128,1024]{1,0:T(8,128)(2,1)S(1)}, u32[]{:S(2)}, u32[]{:S(2)}) %collective-permute-start.9) | collective-permute-done | bytes 262176 | tf_op jit(solution)/shard_map/ppermute | solution.py:260
  76.4 4.6 %collective-permute-start.10 = (bf16[128,1024]{1,0:T(8,128)(2,1)S(1)}, bf16[128,1024]{1,0:T(8,128)(2,1)S(1)}, u32[]{:S(2)}, u32[]{:S(2)}) collective-permute-start(bf16[128,1024]{1,0:T(8,128)(2,1)S(1)} %collective-permute-done.9.refs_3_.refs_4_), channel_id=1, source_target_pairs={{0,1},{1,2},{2,3},{4,5},{5,6},{6,7},{8,9},{9,10},{10,11},{12,13},{... | collective-permute-start | bytes 786440 | tf_op jit(solution)/shard_map/ppermute | solution.py:260
  81.0 1.0 %collective-permute-done.12.refs_4_ = bf16[128,1024]{1,0:T(8,128)(2,1)S(1)} collective-permute-done((bf16[128,1024]{1,0:T(8,128)(2,1)S(1)}, bf16[128,1024]{1,0:T(8,128)(2,1)S(1)}, u32[]{:S(2)}, u32[]{:S(2)}) %collective-permute-start.12) | collective-permute-done | bytes 262176 | tf_op jit(solution)/shard_map/ppermute | solution.py:260
  82.1 3.1 %collective-permute-done.10.refs_5_ = bf16[128,1024]{1,0:T(8,128)(2,1)S(1)} collective-permute-done((bf16[128,1024]{1,0:T(8,128)(2,1)S(1)}, bf16[128,1024]{1,0:T(8,128)(2,1)S(1)}, u32[]{:S(2)}, u32[]{:S(2)}) %collective-permute-start.10) | collective-permute-done | bytes 262176 | tf_op jit(solution)/shard_map/ppermute | solution.py:260
  85.1 3.8 %attend.2.refs_6_ = bf16[256,2048]{1,0:T(8,128)(2,1)} custom-call(f32[256,128]{1,0:T(8,128)S(1)} %get-tuple-element.9.cos_ref, f32[256,128]{1,0:T(8,128)S(1)} %get-tuple-element.10.sin_ref, f32[256,768]{1,0:T(8,128)S(1)} %add_select_fusion.bias_ref, f32[256,3072]{1,0:T(8,128)S(1)} %own_product.1.own_ref, ...), custom_call_target="tpu_custom_call" | custom-call | tf_op jit(solution)/shard_map/attend/pallas_call | solution.py:187
  88.9 3.8 %attend.3 = bf16[256,2048]{1,0:T(8,128)(2,1)} custom-call(f32[256,128]{1,0:T(8,128)S(1)} %get-tuple-element.9.cos_ref, f32[256,128]{1,0:T(8,128)S(1)} %get-tuple-element.10.sin_ref, f32[256,768]{1,0:T(8,128)S(1)} %add_select_fusion.bias_ref, f32[256,3072]{1,0:T(8,128)S(1)} %own_product.1.own_ref, ...), custom_call_target="tpu_custom_call", output_to_operand_aliasing={{}: (10, {})} | custom-call | tf_op jit(solution)/shard_map/attend/pallas_call | solution.py:187
  (28 shorter events, 0.4 us)
Async XLA Ops:
  0.0 15.6 %copy-start.5 = (s32[1,256]{1,0:T(1,128)S(1)}, s32[1,256]{1,0:T(1,128)}, u32[]{:S(2)}) copy-start(s32[1,256]{1,0:T(1,128)} %param.7) | copy-start | bytes 3076
  0.0 37.2 %collective-permute-start.3 = (bf16[1024,3072]{1,0:T(8,128)(2,1)}, bf16[1024,3072]{1,0:T(8,128)(2,1)}, u32[]{:S(2)}, u32[]{:S(2)}) collective-permute-start(bf16[1024,3072]{1,0:T(8,128)(2,1)} %near.9), channel_id=1, source_target_pairs={{0,4},{4,0},{8,12},{12,8},{1,5},{5,1},{9,13},{13,9},{2,6},{6,2},{1... | collective-permute-start | bytes 18874376 | tf_op jit(solution)/shard_map/ppermute | solution.py:220
  0.5 15.1 %collective-permute-start.2 = (s32[1,256]{1,0:T(1,128)}, s32[1,256]{1,0:T(1,128)S(1)}, u32[]{:S(2)}, u32[]{:S(2)}) collective-permute-start(s32[1,256]{1,0:T(1,128)} %param.7), channel_id=1, source_target_pairs={{0,2},{1,3},{4,6},{5,7},{8,10},{9,11},{12,14},{13,15},{16,18},{17,... | collective-permute-start | bytes 3080 | tf_op jit(solution)/shard_map/ppermute | solution.py:241
  6.1 9.5 %collective-permute-start.1 = (s32[1,256]{1,0:T(1,128)}, s32[1,256]{1,0:T(1,128)S(1)}, u32[]{:S(2)}, u32[]{:S(2)}) collective-permute-start(s32[1,256]{1,0:T(1,128)} %param.7), channel_id=1, source_target_pairs={{0,1},{1,2},{2,3},{4,5},{5,6},{6,7},{8,9},{9,10},{10,11},{12,13},{... | collective-permute-start | bytes 3080 | tf_op jit(solution)/shard_map/ppermute | solution.py:241
  9.6 1.6 %copy-start.1 = (bf16[1,256,4096]{2,1,0:T(8,128)(2,1)S(1)}, bf16[1,256,4096]{2,1,0:T(8,128)(2,1)}, u32[]{:S(2)}) copy-start(bf16[1,256,4096]{2,1,0:T(8,128)(2,1)} %param.4) | copy-start | bytes 6291460
  11.2 0.7 copy-start.3
  12.3 32.8 %collective-permute-start = (bf16[128,2048]{1,0:T(8,128)(2,1)S(1)}, bf16[128,2048]{1,0:T(8,128)(2,1)S(1)}, u32[]{:S(2)}, u32[]{:S(2)}) collective-permute-start(bf16[128,2048]{1,0:T(8,128)(2,1)S(1)} %norm_sent.2), channel_id=1, source_target_pairs={{0,8},{4,12},{8,0},{12,4},{1,9},{5,13},{9,1},{13,5},{2,10},{6,14},... | collective-permute-start | bytes 1572872 | tf_op jit(solution)/shard_map/ppermute | solution.py:214
  14.3 23.0 %collective-permute-start.5 = (bf16[128,2048]{1,0:T(8,128)(2,1)S(1)}, bf16[128,2048]{1,0:T(8,128)(2,1)S(1)}, u32[]{:S(2)}, u32[]{:S(2)}) collective-permute-start(bf16[128,2048]{1,0:T(8,128)(2,1)S(1)} %norm_sent.3), channel_id=1, source_target_pairs={{0,8},{4,12},{8,0},{12,4},{1,9},{5,13},{9,1},{13,5},{2,10},{6,14},... | collective-permute-start | bytes 1572872 | tf_op jit(solution)/shard_map/ppermute | solution.py:214
  37.2 2.8 %copy-start = (bf16[1024,3072]{1,0:T(8,128)(2,1)S(1)}, bf16[1024,3072]{1,0:T(8,128)(2,1)}, u32[]{:S(2)}) copy-start(bf16[1024,3072]{1,0:T(8,128)(2,1)} %near.9) | copy-start | bytes 18874372
  43.5 18.2 %collective-permute-start.6 = (bf16[128,1024]{1,0:T(8,128)(2,1)S(1)}, bf16[128,1024]{1,0:T(8,128)(2,1)S(1)}, u32[]{:S(2)}, u32[]{:S(2)}) collective-permute-start(bf16[128,1024]{1,0:T(8,128)(2,1)S(1)} %guest_product.5), channel_id=1, source_target_pairs={{0,8},{4,12},{8,0},{12,4},{1,9},{5,13},{9,1},{13,5},{2,10},{6,14},... | collective-permute-start | bytes 786440 | tf_op jit(solution)/shard_map/ppermute | solution.py:217
  45.1 9.9 %slice-start = ((s8[6291456]{0:T(1024)(128)(4,1)}), s8[4194304]{0:T(1024)(128)(4,1)S(1)}, s32[]{:S(2)}) async-start(s8[6291456]{0:T(1024)(128)(4,1)} %bitcast.5), calls=%async_computation | async-start | bytes 8388608
  48.8 6.3 %slice-start.1 = ((s8[6291456]{0:T(1024)(128)(4,1)}), s8[2097152]{0:T(1024)(128)(4,1)S(1)}, s32[]{:S(2)}) async-start(s8[6291456]{0:T(1024)(128)(4,1)} %bitcast.5), calls=%async_computation.1 | async-start | bytes 4194304
  48.8 6.2 %copy-start.2 = (bf16[1,256,4096]{2,1,0:T(8,128)(2,1)S(1)}, bf16[1,256,4096]{2,1,0:T(8,128)(2,1)}, u32[]{:S(2)}) copy-start(bf16[1,256,4096]{2,1,0:T(8,128)(2,1)} %param.4) | copy-start | bytes 6291460
  48.8 6.2 %copy-start.4 = (bf16[4096]{0:T(1024)(128)(2,1)S(1)}, bf16[4096]{0:T(1024)(128)(2,1)}, u32[]{:S(2)}) copy-start(bf16[4096]{0:T(1024)(128)(2,1)} %gain_ref.5) | copy-start | bytes 24580
  48.8 15.3 %collective-permute-start.7 = (bf16[128,1024]{1,0:T(8,128)(2,1)S(1)}, bf16[128,1024]{1,0:T(8,128)(2,1)S(1)}, u32[]{:S(2)}, u32[]{:S(2)}) collective-permute-start(bf16[128,1024]{1,0:T(8,128)(2,1)S(1)} %guest_product.6), channel_id=1, source_target_pairs={{0,8},{4,12},{8,0},{12,4},{1,9},{5,13},{9,1},{13,5},{2,10},{6,14},... | collective-permute-start | bytes 786440 | tf_op jit(solution)/shard_map/ppermute | solution.py:217
  53.7 27.3 %collective-permute-start.11 = (bf16[128,2048]{1,0:T(8,128)(2,1)S(1)}, bf16[128,2048]{1,0:T(8,128)(2,1)S(1)}, u32[]{:S(2)}, u32[]{:S(2)}) collective-permute-start(bf16[128,2048]{1,0:T(8,128)(2,1)S(1)} %guest_product.7), channel_id=1, source_target_pairs={{0,8},{4,12},{8,0},{12,4},{1,9},{5,13},{9,1},{13,5},{2,10},{6,14},... | collective-permute-start | bytes 1572872 | tf_op jit(solution)/shard_map/ppermute | solution.py:217
  61.9 9.3 %collective-permute-start.8 = (bf16[128,1024]{1,0:T(8,128)(2,1)S(1)}, bf16[128,1024]{1,0:T(8,128)(2,1)S(1)}, u32[]{:S(2)}, u32[]{:S(2)}) collective-permute-start(bf16[128,1024]{1,0:T(8,128)(2,1)S(1)} %finish_kv.2.refs_1_), channel_id=1, source_target_pairs={{0,1},{1,2},{2,3},{4,5},{5,6},{6,7},{8,9},{9,10},{10,11},{12,13},{... | collective-permute-start | bytes 786440 | tf_op jit(solution)/shard_map/ppermute | solution.py:260
  64.3 12.1 %collective-permute-start.9 = (bf16[128,1024]{1,0:T(8,128)(2,1)S(1)}, bf16[128,1024]{1,0:T(8,128)(2,1)S(1)}, u32[]{:S(2)}, u32[]{:S(2)}) collective-permute-start(bf16[128,1024]{1,0:T(8,128)(2,1)S(1)} %finish_kv.3.refs_2_), channel_id=1, source_target_pairs={{0,1},{1,2},{2,3},{4,5},{5,6},{6,7},{8,9},{9,10},{10,11},{12,13},{... | collective-permute-start | bytes 786440 | tf_op jit(solution)/shard_map/ppermute | solution.py:260
  70.3 18.6 %collective-permute-start.4 = (bf16[128,2048]{1,0:T(8,128)(2,1)S(1)}, bf16[128,2048]{1,0:T(8,128)(2,1)S(1)}, u32[]{:S(2)}, u32[]{:S(2)}) collective-permute-start(bf16[128,2048]{1,0:T(8,128)(2,1)S(1)} %guest_product.4), channel_id=1, source_target_pairs={{0,8},{4,12},{8,0},{12,4},{1,9},{5,13},{9,1},{13,5},{2,10},{6,14},... | collective-permute-start | bytes 1572872 | tf_op jit(solution)/shard_map/ppermute | solution.py:217
  71.2 10.9 %collective-permute-start.12 = (bf16[128,1024]{1,0:T(8,128)(2,1)S(1)}, bf16[128,1024]{1,0:T(8,128)(2,1)S(1)}, u32[]{:S(2)}, u32[]{:S(2)}) collective-permute-start(bf16[128,1024]{1,0:T(8,128)(2,1)S(1)} %collective-permute-done.8.refs_2_.refs_3_), channel_id=1, source_target_pairs={{0,1},{1,2},{2,3},{4,5},{5,6},{6,7},{8,9},{9,10},{10,11},{12,13},{... | collective-permute-start | bytes 786440 | tf_op jit(solution)/shard_map/ppermute | solution.py:260
  76.4 8.7 %collective-permute-start.10 = (bf16[128,1024]{1,0:T(8,128)(2,1)S(1)}, bf16[128,1024]{1,0:T(8,128)(2,1)S(1)}, u32[]{:S(2)}, u32[]{:S(2)}) collective-permute-start(bf16[128,1024]{1,0:T(8,128)(2,1)S(1)} %collective-permute-done.9.refs_3_.refs_4_), channel_id=1, source_target_pairs={{0,1},{1,2},{2,3},{4,5},{5,6},{6,7},{8,9},{9,10},{10,11},{12,13},{... | collective-permute-start | bytes 786440 | tf_op jit(solution)/shard_map/ppermute | solution.py:260

commit v4 on v3

--- a/solution.py
+++ b/solution.py
@@ -37,10 +37,8 @@
         out_ref[:, half * depth : (half + 1) * depth] = piece.astype(jnp.bfloat16)
 
 
-def norm_kernel(chips, part, tok_ref, gain_ref, *out_refs):
+def norm_kernel(chips, tok_ref, gain_ref, *out_refs):
     place = lax.axis_index("dp")
-    step = out_refs[0].shape[0]
-    tok_ref = tok_ref.at[pl.ds(part * step, step)]
     scale = row_scale(tok_ref[...].astype(jnp.float32))
     for j, out_ref in enumerate(out_refs, 1):
         chip = lax.rem(lax.div(place, 2) + j, chips)
@@ -48,12 +46,17 @@
 
 
 def norm_sent(rows, gain, part, depth, chips):
-    step = rows.shape[0] // HALVES
-    return pl.pallas_call(
-        functools.partial(norm_kernel, chips, part),
+    tok, width = rows.shape
+    step = tok // HALVES
+    return pl.pallas_call(
+        functools.partial(norm_kernel, chips),
         out_shape=[jax.ShapeDtypeStruct((step, 2 * depth), jnp.bfloat16)] * (chips - 1),
-        in_specs=[VMEM, VMEM],
-        out_specs=[VMEM] * (chips - 1),
+        grid=(1,),
+        in_specs=[
+            pl.BlockSpec((step, width), lambda i: (part, 0)),
+            pl.BlockSpec((width,), lambda i: (0,)),
+        ],
+        out_specs=[pl.BlockSpec((step, 2 * depth), lambda i: (0, 0))] * (chips - 1),
         compiler_params=PARAMS,
         name="norm_sent",
     )(rows, gain)
@@ -68,22 +71,50 @@
         out_ref[:, start : start + tile] = total.astype(out_ref.dtype)
 
 
-def own_kernel(tok_ref, gain_ref, near, far, out_ref, mine):
+def own_kernel(
+    tok_hbm, gain_hbm, near_hbm, far_hbm, out_ref, near, far, tok_ref, gain_ref, mine, sems
+):
+    tile = 512
+    _, columns = near.shape
+    tok_copy = pltpu.make_async_copy(tok_hbm, tok_ref, sems.at[0, columns // tile])
+    tok_copy.start()
+    gain_copy = pltpu.make_async_copy(gain_hbm, gain_ref, sems.at[1, columns // tile])
+    gain_copy.start()
+    copies = []
+    for start in range(0, columns, tile):
+        cut = pl.ds(start, tile)
+        for i, (source, target) in enumerate(((near_hbm, near), (far_hbm, far))):
+            copy = pltpu.make_async_copy(
+                source.at[:, cut], target.at[:, cut], sems.at[i, start // tile]
+            )
+            copy.start()
+            copies.append(copy)
     place = lax.axis_index("dp")
+    tok_copy.wait()
+    gain_copy.wait()
     scale = row_scale(tok_ref[...].astype(jnp.float32))
     write_blocks(tok_ref, gain_ref, scale, mine, lax.div(place, 2), lax.rem(place, 2))
-    multiply(mine, near, far, 0, out_ref)
+    for start in range(0, columns, tile):
+        copies[2 * start // tile].wait()
+        copies[2 * start // tile + 1].wait()
+        multiply(mine, near, far, start, out_ref.at[:, pl.ds(start, tile)])
 
 
 def own_product(rows, gain, near, far):
-    tok = rows.shape[0]
+    tok, width = rows.shape
     depth, columns = near.shape
+    kept = jax.ShapeDtypeStruct(near.shape, near.dtype)
     return pl.pallas_call(
         own_kernel,
-        out_shape=jax.ShapeDtypeStruct((tok, columns), jnp.float32),
-        in_specs=[VMEM] * 4,
-        out_specs=VMEM,
-        scratch_shapes=[pltpu.VMEM((tok, 2 * depth), jnp.bfloat16)],
+        out_shape=[jax.ShapeDtypeStruct((tok, columns), jnp.float32), kept, kept],
+        in_specs=[ANY, ANY, ANY, ANY],
+        out_specs=[VMEM] * 3,
+        scratch_shapes=[
+            pltpu.VMEM((tok, width), jnp.bfloat16),
+            pltpu.VMEM((width,), jnp.bfloat16),
+            pltpu.VMEM((tok, 2 * depth), jnp.bfloat16),
+            pltpu.SemaphoreType.DMA((2, columns // 512 + 1)),
+        ],
         compiler_params=PARAMS,
         name="own_product",
     )(rows, gain, near, far)
@@ -218,9 +249,9 @@
 
     near = qkv_weight
     far = lax.ppermute(qkv_weight, "dp", [(i, i ^ 1) for i in range(ranks)])
-    gain = norm_gain
+    gain = pltpu.with_memory_space_constraint(norm_gain, pltpu.HBM)
+    rows = pltpu.with_memory_space_constraint(tokens[0], pltpu.HBM)
     guests = []
-    rows = tokens[0]
     for part in range(HALVES):
         sent = norm_sent(rows, gain, part, depth, chips)
         guests.append([away(piece, j) for j, piece in enumerate(sent, 1)])
@@ -242,8 +273,8 @@
         allow.append((rank >= hop) & (other[None, :] == docs[:, None]))
     bias = jnp.where(jnp.concatenate(allow, axis=1), 0.0, -1e30).astype(jnp.float32)
 
-    guests[1], bias, cosine, sine = lax.optimization_barrier((guests[1], bias, cosine, sine))
-    own = own_product(rows, gain, near, far)
+    near = pltpu.with_memory_space_constraint(near, pltpu.HBM)
+    own, near, far = own_product(rows, gain, near, far)
 
     kv_got, q_got = [], []
     for part in range(HALVES):

time: 93.3 us -> 85.5 us (0.916)
  waiting for transfers between devices: 26.7 us -> 20.8 us
  local copies, waits for them, and re-layouts: 5.1 us -> 0.01 us
  Pallas kernels: 31 us -> 32.8 us
  starting transfers between devices: 28.8 us -> 30.1 us
    ppermute x2, waiting for transfers between devices: 21.3 us -> 8.47 us  [away(): lax.ppermute(part, 'dp', [(i, (i + 2 * j) % ranks) for i in range(ranks)])]
    pallas_call x4, Pallas kernels: 15.5 us -> 9.74 us  [guest_product(): pl.pallas_call(functools.partial(guest_kernel, first), out_shape=jax.Shap...]
    unnamed x16 -> x2, local copies, waits for them, and re-layouts: 5.1 us -> 0.01 us
    pallas_call x3, Pallas kernels: 7.53 us -> 11.6 us  [the longest x1 6.77 us: own_product(): pl.pallas_call(own_kernel, out_shape=[jax.ShapeDtypeStruct((tok, columns)...]
    ppermute x1, waiting for transfers between devices: 0.01 us -> 2.75 us  [local(): far = lax.ppermute(qkv_weight, 'dp', [(i, i ^ 1) for i in range(ranks)])]
    pallas_call x2, Pallas kernels: 7.59 us -> 9.72 us  [attend(): pl.pallas_call(functools.partial(attend_kernel, part, len(got), picks), o...]
    ppermute x4, waiting for transfers between devices: 5.31 us -> 7.27 us  [local(): lax.ppermute(chunks[part], 'seq', [(i, i + 1) for i in range(count - 1)])]
    ppermute x4, starting transfers between devices: 4.32 us -> 6.2 us  [home(): lax.ppermute(part, 'dp', [(i, (i - 2 * j) % ranks) for i in range(ranks)])]
  transfers between devices with their start and end apart: 13 -> 13, of which waited for: 4 -> 7; matrix products, arithmetic and copies ran while one was open for 1% -> 1% of each run, Pallas kernels for 29% -> 33%
where the time goes in v4:
time: 85.5 us; the launch traced here: 85 us
  Pallas kernels  32.8 us (38%)
  starting transfers between devices  30.1 us (35%)
  waiting for transfers between devices  20.8 us (24%)
  other arithmetic  0.96 us (1%)
    ppermute x4, starting transfers between devices, local(): lax.ppermute(chunks[part], 'seq', [(i, i + 1) for i in range(count - 1)])  13 us
    pallas_call x4, Pallas kernels, guest_product(): pl.pallas_call(functools.partial(guest_kernel, first), out_shape=jax.Shap...  9.74 us
    pallas_call x2, Pallas kernels, attend(): pl.pallas_call(functools.partial(attend_kernel, part, len(got), picks), o...  9.72 us
    ppermute x2, waiting for transfers between devices, away(): lax.ppermute(part, 'dp', [(i, (i + 2 * j) % ranks) for i in range(ranks)])  8.47 us
    ppermute x2, starting transfers between devices, local(): lax.ppermute(doc_ids, 'seq', [(i, i + hop) for i in range(count - hop)])[0]  7.95 us
    ppermute x4, waiting for transfers between devices, local(): lax.ppermute(chunks[part], 'seq', [(i, i + 1) for i in range(count - 1)])  7.27 us
    pallas_call x1, Pallas kernels, own_product(): pl.pallas_call(own_kernel, out_shape=[jax.ShapeDtypeStruct((tok, columns)...  6.77 us
    ppermute x4, starting transfers between devices, home(): lax.ppermute(part, 'dp', [(i, (i - 2 * j) % ranks) for i in range(ranks)])  6.2 us
  transfers between devices with their start and end apart: 13, of which 7 were waited for; matrix products, arithmetic and copies ran while one was open for 1% of the time, Pallas kernels for 33%

profile of v4, /device:TPU:0, one launch (start us, length us, event | category | flops | bytes accessed | tf_op | source)
XLA Modules:
  0.0 85.0 jit_solution(7651210175571080609)
XLA Ops:
  0.0 0.5 collective-permute-start.2
  0.5 2.4 %norm_sent.2 = bf16[128,2048]{1,0:T(8,128)(2,1)} custom-call(bf16[256,4096]{1,0:T(8,128)(2,1)} %bitcast.5, bf16[4096]{0:T(1024)(128)(2,1)} %gain_ref.3), custom_call_target="tpu_custom_call" | custom-call | tf_op jit(solution)/shard_map/norm_sent/pallas_call | solution.py:51
  2.9 2.5 %collective-permute-start.3 = (bf16[128,2048]{1,0:T(8,128)(2,1)}, bf16[128,2048]{1,0:T(8,128)(2,1)}, u32[]{:S(2)}, u32[]{:S(2)}) collective-permute-start(bf16[128,2048]{1,0:T(8,128)(2,1)} %norm_sent.2), channel_id=1, source_target_pairs={{0,8},{4,12},{8,0},{12,4},{1,9},{5,13},{9,1},{13,5},{2,10},{6,14},... | collective-permute-start | bytes 1572872 | tf_op jit(solution)/shard_map/ppermute | solution.py:245
  5.4 2.4 %norm_sent.3 = bf16[128,2048]{1,0:T(8,128)(2,1)} custom-call(bf16[256,4096]{1,0:T(8,128)(2,1)} %bitcast.6, bf16[4096]{0:T(1024)(128)(2,1)} %gain_ref.3), custom_call_target="tpu_custom_call" | custom-call | tf_op jit(solution)/shard_map/norm_sent/pallas_call | solution.py:51
  7.9 2.8 %collective-permute-done.2.far_hbm = bf16[1024,3072]{1,0:T(8,128)(2,1)} collective-permute-done((bf16[1024,3072]{1,0:T(8,128)(2,1)}, bf16[1024,3072]{1,0:T(8,128)(2,1)}, u32[]{:S(2)}, u32[]{:S(2)}) %collective-permute-start.2) | collective-permute-done | bytes 6291488 | tf_op jit(solution)/shard_map/ppermute | solution.py:251
  10.6 6.8 %own_product.1 = (f32[256,3072]{1,0:T(8,128)S(1)}, bf16[1024,3072]{1,0:T(8,128)(2,1)S(1)}, bf16[1024,3072]{1,0:T(8,128)(2,1)S(1)}) custom-call(bf16[256,4096]{1,0:T(8,128)(2,1)} %bitcast.7, bf16[4096]{0:T(1024)(128)(2,1)} %gain_ref.3, bf16[1024,3072]{1,0:T(8,128)(2,1)} %near_hbm.1, bf16[1024,3072]{1,0:T(8,128)(2,1)} %collective-permute-done.2.far_hbm), custom_call_target="tpu_custom_call" | custom-call | tf_op jit(solution)/shard_map/own_product/pallas_call | solution.py:107
  17.4 1.1 %collective-permute-done.3.rows = bf16[128,2048]{1,0:T(8,128)(2,1)} collective-permute-done((bf16[128,2048]{1,0:T(8,128)(2,1)}, bf16[128,2048]{1,0:T(8,128)(2,1)}, u32[]{:S(2)}, u32[]{:S(2)}) %collective-permute-start.3) | collective-permute-done | bytes 524320 | tf_op jit(solution)/shard_map/ppermute | solution.py:245
  18.5 1.8 %guest_product.6 = bf16[128,1024]{1,0:T(8,128)(2,1)S(1)} custom-call(bf16[128,2048]{1,0:T(8,128)(2,1)} %collective-permute-done.3.rows, bf16[1024,3072]{1,0:T(8,128)(2,1)S(1)} %get-tuple-element.9.near, bf16[1024,3072]{1,0:T(8,128)(2,1)S(1)} %get-tuple-element.10.far), custom_call_target="tpu_custom_call" | custom-call | tf_op jit(solution)/shard_map/guest_product/pallas_call | solution.py:128
  20.3 2.1 %collective-permute-start.7 = (bf16[128,1024]{1,0:T(8,128)(2,1)S(1)}, bf16[128,1024]{1,0:T(8,128)(2,1)S(1)}, u32[]{:S(2)}, u32[]{:S(2)}) collective-permute-start(bf16[128,1024]{1,0:T(8,128)(2,1)S(1)} %guest_product.6), channel_id=1, source_target_pairs={{0,8},{4,12},{8,0},{12,4},{1,9},{5,13},{9,1},{13,5},{2,10},{6,14},... | collective-permute-start | bytes 786440 | tf_op jit(solution)/shard_map/ppermute | solution.py:248
  22.4 7.4 %collective-permute-done.5.rows = bf16[128,2048]{1,0:T(8,128)(2,1)} collective-permute-done((bf16[128,2048]{1,0:T(8,128)(2,1)}, bf16[128,2048]{1,0:T(8,128)(2,1)}, u32[]{:S(2)}, u32[]{:S(2)}) %collective-permute-start.5) | collective-permute-done | bytes 524320 | tf_op jit(solution)/shard_map/ppermute | solution.py:245
  29.7 1.8 %guest_product.5 = bf16[128,1024]{1,0:T(8,128)(2,1)S(1)} custom-call(bf16[128,2048]{1,0:T(8,128)(2,1)} %collective-permute-done.5.rows, bf16[1024,3072]{1,0:T(8,128)(2,1)S(1)} %get-tuple-element.9.near, bf16[1024,3072]{1,0:T(8,128)(2,1)S(1)} %get-tuple-element.10.far), custom_call_target="tpu_custom_call" | custom-call | tf_op jit(solution)/shard_map/guest_product/pallas_call | solution.py:128
  31.5 2.1 %collective-permute-start.6 = (bf16[128,1024]{1,0:T(8,128)(2,1)S(1)}, bf16[128,1024]{1,0:T(8,128)(2,1)S(1)}, u32[]{:S(2)}, u32[]{:S(2)}) collective-permute-start(bf16[128,1024]{1,0:T(8,128)(2,1)S(1)} %guest_product.5), channel_id=1, source_target_pairs={{0,8},{4,12},{8,0},{12,4},{1,9},{5,13},{9,1},{13,5},{2,10},{6,14},... | collective-permute-start | bytes 786440 | tf_op jit(solution)/shard_map/ppermute | solution.py:248
  33.6 0.5 fusion.1
  34.3 1.0 %collective-permute-done.7.refs_0_ = bf16[128,1024]{1,0:T(8,128)(2,1)S(1)} collective-permute-done((bf16[128,1024]{1,0:T(8,128)(2,1)S(1)}, bf16[128,1024]{1,0:T(8,128)(2,1)S(1)}, u32[]{:S(2)}, u32[]{:S(2)}) %collective-permute-start.7) | collective-permute-done | bytes 262176 | tf_op jit(solution)/shard_map/ppermute | solution.py:248
  35.2 0.9 %finish_kv.3.refs_2_ = bf16[128,1024]{1,0:T(8,128)(2,1)} custom-call(f32[256,128]{1,0:T(8,128)S(1)} %get-tuple-element.17.cos_ref, f32[256,128]{1,0:T(8,128)S(1)} %get-tuple-element.18.sin_ref, f32[256,3072]{1,0:T(8,128)S(1)} %get-tuple-element.8.own_ref, bf16[128,1024]{1,0:T(8,128)(2,1)S(1)} %collective-permute-done.7.refs_0_), custom_call_target="tpu_custom_call" | custom-call | tf_op jit(solution)/shard_map/finish_kv/pallas_call | solution.py:158
  36.1 4.7 %collective-permute-start.9 = (bf16[128,1024]{1,0:T(8,128)(2,1)}, bf16[128,1024]{1,0:T(8,128)(2,1)}, u32[]{:S(2)}, u32[]{:S(2)}) collective-permute-start(bf16[128,1024]{1,0:T(8,128)(2,1)} %finish_kv.3.refs_2_), channel_id=1, source_target_pairs={{0,1},{1,2},{2,3},{4,5},{5,6},{6,7},{8,9},{9,10},{10,11},{12,13},{... | collective-permute-start | bytes 786440 | tf_op jit(solution)/shard_map/ppermute | solution.py:291
  40.9 0.9 %finish_kv.2.refs_1_ = bf16[128,1024]{1,0:T(8,128)(2,1)} custom-call(f32[256,128]{1,0:T(8,128)S(1)} %get-tuple-element.17.cos_ref, f32[256,128]{1,0:T(8,128)S(1)} %get-tuple-element.18.sin_ref, f32[256,3072]{1,0:T(8,128)S(1)} %get-tuple-element.8.own_ref, bf16[128,1024]{1,0:T(8,128)(2,1)S(1)} %collective-permute-done.6.refs_0_), custom_call_target="tpu_custom_call" | custom-call | tf_op jit(solution)/shard_map/finish_kv/pallas_call | solution.py:158
  41.7 4.3 %collective-permute-start.8 = (bf16[128,1024]{1,0:T(8,128)(2,1)}, bf16[128,1024]{1,0:T(8,128)(2,1)}, u32[]{:S(2)}, u32[]{:S(2)}) collective-permute-start(bf16[128,1024]{1,0:T(8,128)(2,1)} %finish_kv.2.refs_1_), channel_id=1, source_target_pairs={{0,1},{1,2},{2,3},{4,5},{5,6},{6,7},{8,9},{9,10},{10,11},{12,13},{... | collective-permute-start | bytes 786440 | tf_op jit(solution)/shard_map/ppermute | solution.py:291
  46.0 3.1 %guest_product.7 = bf16[128,2048]{1,0:T(8,128)(2,1)} custom-call(bf16[128,2048]{1,0:T(8,128)(2,1)} %collective-permute-done.5.rows, bf16[1024,3072]{1,0:T(8,128)(2,1)S(1)} %get-tuple-element.9.near, bf16[1024,3072]{1,0:T(8,128)(2,1)S(1)} %get-tuple-element.10.far), custom_call_target="tpu_custom_call" | custom-call | tf_op jit(solution)/shard_map/guest_product/pallas_call | solution.py:128
  49.1 1.5 %collective-permute-start.11 = (bf16[128,2048]{1,0:T(8,128)(2,1)}, bf16[128,2048]{1,0:T(8,128)(2,1)}, u32[]{:S(2)}, u32[]{:S(2)}) collective-permute-start(bf16[128,2048]{1,0:T(8,128)(2,1)} %guest_product.7), channel_id=1, source_target_pairs={{0,8},{4,12},{8,0},{12,4},{1,9},{5,13},{9,1},{13,5},{2,10},{6,14},... | collective-permute-start | bytes 1572872 | tf_op jit(solution)/shard_map/ppermute | solution.py:248
  50.6 3.1 %guest_product.4 = bf16[128,2048]{1,0:T(8,128)(2,1)} custom-call(bf16[128,2048]{1,0:T(8,128)(2,1)} %collective-permute-done.3.rows, bf16[1024,3072]{1,0:T(8,128)(2,1)S(1)} %get-tuple-element.9.near, bf16[1024,3072]{1,0:T(8,128)(2,1)S(1)} %get-tuple-element.10.far), custom_call_target="tpu_custom_call" | custom-call | tf_op jit(solution)/shard_map/guest_product/pallas_call | solution.py:128
  53.7 0.5 collective-permute-start.4
  54.2 2.8 %collective-permute-start = (s32[1,256]{1,0:T(1,128)S(1)}, s32[1,256]{1,0:T(1,128)S(1)}, u32[]{:S(2)}, u32[]{:S(2)}) collective-permute-start(s32[1,256]{1,0:T(1,128)S(1)} %copy-done), channel_id=1, source_target_pairs={{0,1},{1,2},{2,3},{4,5},{5,6},{6,7},{8,9},{9,10},{10,11},{12,13},{... | collective-permute-start | bytes 3080 | tf_op jit(solution)/shard_map/ppermute | solution.py:272
  57.0 1.3 %collective-permute-done = s32[1,256]{1,0:T(1,128)S(1)} collective-permute-done((s32[1,256]{1,0:T(1,128)S(1)}, s32[1,256]{1,0:T(1,128)S(1)}, u32[]{:S(2)}, u32[]{:S(2)}) %collective-permute-start) | collective-permute-done | bytes 1056 | tf_op jit(solution)/shard_map/ppermute | solution.py:272
  58.3 5.2 %collective-permute-start.1 = (s32[1,256]{1,0:T(1,128)S(1)}, s32[1,256]{1,0:T(1,128)S(1)}, u32[]{:S(2)}, u32[]{:S(2)}) collective-permute-start(s32[1,256]{1,0:T(1,128)S(1)} %copy-done), channel_id=1, source_target_pairs={{0,2},{1,3},{4,6},{5,7},{8,10},{9,11},{12,14},{13,15},{16,18},{17,... | collective-permute-start | bytes 3080 | tf_op jit(solution)/shard_map/ppermute | solution.py:272
  63.5 1.9 %collective-permute-start.10 = (bf16[128,1024]{1,0:T(8,128)(2,1)}, bf16[128,1024]{1,0:T(8,128)(2,1)S(1)}, u32[]{:S(2)}, u32[]{:S(2)}) collective-permute-start(bf16[128,1024]{1,0:T(8,128)(2,1)} %collective-permute-done.9.refs_3_.refs_4_), channel_id=1, source_target_pairs={{0,1},{1,2},{2,3},{4,5},{5,6},{6,7},{8,9},{9,10},{10,11},{12,13},{... | collective-permute-start | bytes 786440 | tf_op jit(solution)/shard_map/ppermute | solution.py:291
  65.4 2.1 %collective-permute-start.12 = (bf16[128,1024]{1,0:T(8,128)(2,1)}, bf16[128,1024]{1,0:T(8,128)(2,1)S(1)}, u32[]{:S(2)}, u32[]{:S(2)}) collective-permute-start(bf16[128,1024]{1,0:T(8,128)(2,1)} %collective-permute-done.8.refs_2_.refs_3_), channel_id=1, source_target_pairs={{0,1},{1,2},{2,3},{4,5},{5,6},{6,7},{8,9},{9,10},{10,11},{12,13},{... | collective-permute-start | bytes 786440 | tf_op jit(solution)/shard_map/ppermute | solution.py:291
  67.6 0.2 fusion
  67.9 4.5 %collective-permute-done.10.refs_5_ = bf16[128,1024]{1,0:T(8,128)(2,1)S(1)} collective-permute-done((bf16[128,1024]{1,0:T(8,128)(2,1)}, bf16[128,1024]{1,0:T(8,128)(2,1)S(1)}, u32[]{:S(2)}, u32[]{:S(2)}) %collective-permute-start.10) | collective-permute-done | bytes 262176 | tf_op jit(solution)/shard_map/ppermute | solution.py:291
  72.3 2.8 %collective-permute-done.12.refs_4_ = bf16[128,1024]{1,0:T(8,128)(2,1)S(1)} collective-permute-done((bf16[128,1024]{1,0:T(8,128)(2,1)}, bf16[128,1024]{1,0:T(8,128)(2,1)S(1)}, u32[]{:S(2)}, u32[]{:S(2)}) %collective-permute-start.12) | collective-permute-done | bytes 262176 | tf_op jit(solution)/shard_map/ppermute | solution.py:291
  75.1 4.8 %attend.2.refs_6_ = bf16[256,2048]{1,0:T(8,128)(2,1)} custom-call(f32[256,128]{1,0:T(8,128)S(1)} %get-tuple-element.17.cos_ref, f32[256,128]{1,0:T(8,128)S(1)} %get-tuple-element.18.sin_ref, f32[256,768]{1,0:T(8,128)S(1)} %add_select_fusion.bias_ref, f32[256,3072]{1,0:T(8,128)S(1)} %get-tuple-element.8.own_ref, ...), custom_call_target="tpu_custom_call" | custom-call | tf_op jit(solution)/shard_map/attend/pallas_call | solution.py:218
  80.0 4.9 %attend.3 = bf16[256,2048]{1,0:T(8,128)(2,1)} custom-call(f32[256,128]{1,0:T(8,128)S(1)} %get-tuple-element.17.cos_ref, f32[256,128]{1,0:T(8,128)S(1)} %get-tuple-element.18.sin_ref, f32[256,768]{1,0:T(8,128)S(1)} %add_select_fusion.bias_ref, f32[256,3072]{1,0:T(8,128)S(1)} %get-tuple-element.8.own_ref, ...), custom_call_target="tpu_custom_call", output_to_operand_aliasing={{}: (10, {})} | custom-call | tf_op jit(solution)/shard_map/attend/pallas_call | solution.py:218
  (13 shorter events, 0.3 us)
Async XLA Ops:
  0.0 10.6 %collective-permute-start.2 = (bf16[1024,3072]{1,0:T(8,128)(2,1)}, bf16[1024,3072]{1,0:T(8,128)(2,1)}, u32[]{:S(2)}, u32[]{:S(2)}) collective-permute-start(bf16[1024,3072]{1,0:T(8,128)(2,1)} %near_hbm.1), channel_id=1, source_target_pairs={{0,4},{4,0},{8,12},{12,8},{1,5},{5,1},{9,13},{13,9},{2,6},{6,2},{1... | collective-permute-start | bytes 18874376 | tf_op jit(solution)/shard_map/ppermute | solution.py:251
  2.9 15.6 %collective-permute-start.3 = (bf16[128,2048]{1,0:T(8,128)(2,1)}, bf16[128,2048]{1,0:T(8,128)(2,1)}, u32[]{:S(2)}, u32[]{:S(2)}) collective-permute-start(bf16[128,2048]{1,0:T(8,128)(2,1)} %norm_sent.2), channel_id=1, source_target_pairs={{0,8},{4,12},{8,0},{12,4},{1,9},{5,13},{9,1},{13,5},{2,10},{6,14},... | collective-permute-start | bytes 1572872 | tf_op jit(solution)/shard_map/ppermute | solution.py:245
  7.8 21.9 %collective-permute-start.5 = (bf16[128,2048]{1,0:T(8,128)(2,1)}, bf16[128,2048]{1,0:T(8,128)(2,1)}, u32[]{:S(2)}, u32[]{:S(2)}) collective-permute-start(bf16[128,2048]{1,0:T(8,128)(2,1)} %norm_sent.3), channel_id=1, source_target_pairs={{0,8},{4,12},{8,0},{12,4},{1,9},{5,13},{9,1},{13,5},{2,10},{6,14},... | collective-permute-start | bytes 1572872 | tf_op jit(solution)/shard_map/ppermute | solution.py:245
  20.3 15.0 %collective-permute-start.7 = (bf16[128,1024]{1,0:T(8,128)(2,1)S(1)}, bf16[128,1024]{1,0:T(8,128)(2,1)S(1)}, u32[]{:S(2)}, u32[]{:S(2)}) collective-permute-start(bf16[128,1024]{1,0:T(8,128)(2,1)S(1)} %guest_product.6), channel_id=1, source_target_pairs={{0,8},{4,12},{8,0},{12,4},{1,9},{5,13},{9,1},{13,5},{2,10},{6,14},... | collective-permute-start | bytes 786440 | tf_op jit(solution)/shard_map/ppermute | solution.py:248
  31.5 9.3 %collective-permute-start.6 = (bf16[128,1024]{1,0:T(8,128)(2,1)S(1)}, bf16[128,1024]{1,0:T(8,128)(2,1)S(1)}, u32[]{:S(2)}, u32[]{:S(2)}) collective-permute-start(bf16[128,1024]{1,0:T(8,128)(2,1)S(1)} %guest_product.5), channel_id=1, source_target_pairs={{0,8},{4,12},{8,0},{12,4},{1,9},{5,13},{9,1},{13,5},{2,10},{6,14},... | collective-permute-start | bytes 786440 | tf_op jit(solution)/shard_map/ppermute | solution.py:248
  36.1 27.3 %collective-permute-start.9 = (bf16[128,1024]{1,0:T(8,128)(2,1)}, bf16[128,1024]{1,0:T(8,128)(2,1)}, u32[]{:S(2)}, u32[]{:S(2)}) collective-permute-start(bf16[128,1024]{1,0:T(8,128)(2,1)} %finish_kv.3.refs_2_), channel_id=1, source_target_pairs={{0,1},{1,2},{2,3},{4,5},{5,6},{6,7},{8,9},{9,10},{10,11},{12,13},{... | collective-permute-start | bytes 786440 | tf_op jit(solution)/shard_map/ppermute | solution.py:291
  41.7 23.7 %collective-permute-start.8 = (bf16[128,1024]{1,0:T(8,128)(2,1)}, bf16[128,1024]{1,0:T(8,128)(2,1)}, u32[]{:S(2)}, u32[]{:S(2)}) collective-permute-start(bf16[128,1024]{1,0:T(8,128)(2,1)} %finish_kv.2.refs_1_), channel_id=1, source_target_pairs={{0,1},{1,2},{2,3},{4,5},{5,6},{6,7},{8,9},{9,10},{10,11},{12,13},{... | collective-permute-start | bytes 786440 | tf_op jit(solution)/shard_map/ppermute | solution.py:291
  49.1 5.1 %copy-start = (s32[1,256]{1,0:T(1,128)S(1)}, s32[1,256]{1,0:T(1,128)}, u32[]{:S(2)}) copy-start(s32[1,256]{1,0:T(1,128)} %param.7) | copy-start | bytes 3076
  49.1 18.8 %collective-permute-start.11 = (bf16[128,2048]{1,0:T(8,128)(2,1)}, bf16[128,2048]{1,0:T(8,128)(2,1)}, u32[]{:S(2)}, u32[]{:S(2)}) collective-permute-start(bf16[128,2048]{1,0:T(8,128)(2,1)} %guest_product.7), channel_id=1, source_target_pairs={{0,8},{4,12},{8,0},{12,4},{1,9},{5,13},{9,1},{13,5},{2,10},{6,14},... | collective-permute-start | bytes 1572872 | tf_op jit(solution)/shard_map/ppermute | solution.py:248
  53.7 26.3 %collective-permute-start.4 = (bf16[128,2048]{1,0:T(8,128)(2,1)}, bf16[128,2048]{1,0:T(8,128)(2,1)}, u32[]{:S(2)}, u32[]{:S(2)}) collective-permute-start(bf16[128,2048]{1,0:T(8,128)(2,1)} %guest_product.4), channel_id=1, source_target_pairs={{0,8},{4,12},{8,0},{12,4},{1,9},{5,13},{9,1},{13,5},{2,10},{6,14},... | collective-permute-start | bytes 1572872 | tf_op jit(solution)/shard_map/ppermute | solution.py:248
  54.2 4.1 %collective-permute-start = (s32[1,256]{1,0:T(1,128)S(1)}, s32[1,256]{1,0:T(1,128)S(1)}, u32[]{:S(2)}, u32[]{:S(2)}) collective-permute-start(s32[1,256]{1,0:T(1,128)S(1)} %copy-done), channel_id=1, source_target_pairs={{0,1},{1,2},{2,3},{4,5},{5,6},{6,7},{8,9},{9,10},{10,11},{12,13},{... | collective-permute-start | bytes 3080 | tf_op jit(solution)/shard_map/ppermute | solution.py:272
  58.3 9.3 %collective-permute-start.1 = (s32[1,256]{1,0:T(1,128)S(1)}, s32[1,256]{1,0:T(1,128)S(1)}, u32[]{:S(2)}, u32[]{:S(2)}) collective-permute-start(s32[1,256]{1,0:T(1,128)S(1)} %copy-done), channel_id=1, source_target_pairs={{0,2},{1,3},{4,6},{5,7},{8,10},{9,11},{12,14},{13,15},{16,18},{17,... | collective-permute-start | bytes 3080 | tf_op jit(solution)/shard_map/ppermute | solution.py:272
  63.5 8.8 %collective-permute-start.10 = (bf16[128,1024]{1,0:T(8,128)(2,1)}, bf16[128,1024]{1,0:T(8,128)(2,1)S(1)}, u32[]{:S(2)}, u32[]{:S(2)}) collective-permute-start(bf16[128,1024]{1,0:T(8,128)(2,1)} %collective-permute-done.9.refs_3_.refs_4_), channel_id=1, source_target_pairs={{0,1},{1,2},{2,3},{4,5},{5,6},{6,7},{8,9},{9,10},{10,11},{12,13},{... | collective-permute-start | bytes 786440 | tf_op jit(solution)/shard_map/ppermute | solution.py:291
  65.4 9.7 %collective-permute-start.12 = (bf16[128,1024]{1,0:T(8,128)(2,1)}, bf16[128,1024]{1,0:T(8,128)(2,1)S(1)}, u32[]{:S(2)}, u32[]{:S(2)}) collective-permute-start(bf16[128,1024]{1,0:T(8,128)(2,1)} %collective-permute-done.8.refs_2_.refs_3_), channel_id=1, source_target_pairs={{0,1},{1,2},{2,3},{4,5},{5,6},{6,7},{8,9},{9,10},{10,11},{12,13},{... | collective-permute-start | bytes 786440 | tf_op jit(solution)/shard_map/ppermute | solution.py:291
